TPU v7x, 32 devices: a whole 2x2x4 slice. The times are simulated.
32 devices in a mesh: prompt: 4 (over z), tensor: 8 (over y, x, core).
Axes of the slice: x: 2, y: 2, z: 4, core: 2. Of those that a mesh axis runs over, the one named last changes fastest.
Arguments:
- embeds: bfloat16 [4, 64, 8192], P('prompt', None, 'tensor'), may hold values from -400 to 400
- norm_gain: bfloat16 [8192], replicated, may hold values from 0.5 to 1.5
- query_weight: bfloat16 [8192, 8192], P('prompt', 'tensor'), may hold values from -1 to 1
- key_weight: bfloat16 [8192, 1024], P('prompt', 'tensor'), may hold values from -6 to 6
- value_weight: bfloat16 [8192, 1024], P('prompt', 'tensor'), may hold values from -0.0625 to 0.0625
- out_weight: bfloat16 [8192, 8192], P('tensor', 'prompt'), may hold values from -0.0625 to 0.0625
- out_grad: bfloat16 [4, 64, 8192], P('prompt', None, 'tensor'), may hold values from -6 to 6
- suffix_pos: int32 [4, 20], P('prompt'), may hold values from 0 to 63
- vocab_table: bfloat16 [65536, 8192], P(('prompt', 'tensor')), may hold values from -0.0625 to 0.0625
- banned: int32 [65536], P(('prompt', 'tensor')), may hold values 0 or 1
Outputs:
- token_scores: float32 [4, 20, 65536], P(None, None, ('prompt', 'tensor'))
All inputs are finite; a program needn't handle non-finite values. No bound on the sum of `banned` on one device may be relied on, other than what follows from the above.
Results may differ from a plain program's by a relative error of at most 0.01.
The roundings to bfloat16 on the way count: a program that leaves them out, or rounds other values in their place, can miss the bound.
Values may be sent and summed in bfloat16 or wider, within the bound.
A program may use at most 192 MiB of HBM per device.

v0:
```python
import math

import jax
import jax.numpy as jnp
from jax import lax
from jax.sharding import PartitionSpec as P

KVH = 8
HD = 128


EPSILON = 1e-05


def on_device(
    embeds,
    norm_gain,
    query_weight,
    key_weight,
    value_weight,
    out_weight,
    out_grad,
    suffix_pos,
    vocab_table,
    banned,
):
    n_tensor = lax.axis_size("tensor")
    suffix_count = suffix_pos.shape[1]
    query_full, key_full, value_full, out_full = (
        lax.all_gather(query_weight, "prompt", axis=0, tiled=True),
        lax.all_gather(key_weight, "prompt", axis=0, tiled=True),
        lax.all_gather(value_weight, "prompt", axis=0, tiled=True),
        lax.all_gather(out_weight, "prompt", axis=1, tiled=True),
    )
    embeds, out_grad = (
        lax.all_gather(embeds, "tensor", axis=2, tiled=True),
        lax.all_gather(out_grad, "tensor", axis=2, tiled=True),
    )
    local_prompts, seq_len, width = embeds.shape
    head_cols = query_full.shape[1]
    heads_here = head_cols // HD
    logit_scale = 1.0 / math.sqrt(HD)
    embeds_float = embeds.astype(jnp.float32)
    inverse_norm = lax.rsqrt(
        jnp.mean(embeds_float * embeds_float, axis=-1, keepdims=True) + EPSILON
    )
    gain_float = norm_gain.astype(jnp.float32)
    normed = (embeds_float * inverse_norm * gain_float).astype(jnp.bfloat16)
    queries = jnp.einsum(
        "psd,dc->psc", normed, query_full, preferred_element_type=jnp.float32
    ).astype(jnp.bfloat16)
    key_part = jnp.einsum(
        "psd,dc->psc", normed, key_full, preferred_element_type=jnp.float32
    ).astype(jnp.bfloat16)
    value_part = jnp.einsum(
        "psd,dc->psc", normed, value_full, preferred_element_type=jnp.float32
    ).astype(jnp.bfloat16)
    keys_all, values_all = (
        lax.all_gather(key_part, "tensor", axis=2, tiled=True),
        lax.all_gather(value_part, "tensor", axis=2, tiled=True),
    )
    first_head = lax.axis_index("tensor") * heads_here
    owners = (first_head + jnp.arange(heads_here, dtype=jnp.int32)) % KVH
    picker = owners[:, None] == jnp.arange(KVH, dtype=jnp.int32)[None, :]
    picker_low = picker.astype(jnp.bfloat16)
    picker_float = picker.astype(jnp.float32)
    key_heads = jnp.einsum(
        "pskd,hk->pshd",
        keys_all.reshape(local_prompts, seq_len, KVH, HD),
        picker_low,
        preferred_element_type=jnp.float32,
    ).astype(jnp.bfloat16)
    value_heads = jnp.einsum(
        "pskd,hk->pshd",
        values_all.reshape(local_prompts, seq_len, KVH, HD),
        picker_low,
        preferred_element_type=jnp.float32,
    ).astype(jnp.bfloat16)
    query_heads = queries.reshape(local_prompts, seq_len, heads_here, HD)
    logits = (
        jnp.einsum("pqhd,pkhd->phqk", query_heads, key_heads, preferred_element_type=jnp.float32)
        * logit_scale
    )
    row_index = lax.broadcasted_iota(jnp.int32, (seq_len, seq_len), 0)
    col_index = lax.broadcasted_iota(jnp.int32, (seq_len, seq_len), 1)
    causal = col_index <= row_index
    largest = jnp.max(jnp.where(causal, logits, -1e30), axis=-1, keepdims=True)
    raised = jnp.where(causal, jnp.exp(logits - largest), 0.0)
    probs_float = raised / jnp.sum(raised, axis=-1, keepdims=True)
    probs_low = probs_float.astype(jnp.bfloat16)
    context_grad = jnp.einsum(
        "psd,cd->psc", out_grad, out_full, preferred_element_type=jnp.float32
    ).astype(jnp.bfloat16)
    context_heads = context_grad.reshape(local_prompts, seq_len, heads_here, HD)
    prob_grad = jnp.einsum(
        "pqhd,pkhd->phqk", context_heads, value_heads, preferred_element_type=jnp.float32
    )
    logit_grad = (
        probs_float
        * (prob_grad - jnp.sum(prob_grad * probs_float, axis=-1, keepdims=True))
        * logit_scale
    ).astype(jnp.bfloat16)
    steps_iota = lax.broadcasted_iota(jnp.int32, (local_prompts, suffix_count, seq_len), 2)
    chooser = (steps_iota == suffix_pos[:, :, None]).astype(jnp.bfloat16)
    logit_rows = jnp.einsum(
        "pns,phsk->phnk", chooser, logit_grad, preferred_element_type=jnp.float32
    ).astype(jnp.bfloat16)
    query_grad = jnp.einsum(
        "phnk,pkhd->pnhd", logit_rows, key_heads, preferred_element_type=jnp.float32
    ).astype(jnp.bfloat16)
    query_grad = query_grad.reshape(local_prompts, suffix_count, head_cols)
    logit_cols = jnp.einsum(
        "phqk,pnk->phnq", logit_grad, chooser, preferred_element_type=jnp.float32
    ).astype(jnp.bfloat16)
    key_each = jnp.einsum(
        "phnq,pqhd->pnhd", logit_cols, query_heads, preferred_element_type=jnp.float32
    )
    prob_cols = jnp.einsum(
        "phqk,pnk->phnq", probs_low, chooser, preferred_element_type=jnp.float32
    ).astype(jnp.bfloat16)
    value_each = jnp.einsum(
        "phnq,pqhd->pnhd", prob_cols, context_heads, preferred_element_type=jnp.float32
    )
    key_slots = jnp.einsum(
        "pnhd,hk->pnkd", key_each, picker_float, precision=lax.Precision.HIGHEST
    ).reshape(local_prompts, suffix_count, KVH * HD)
    value_slots = jnp.einsum(
        "pnhd,hk->pnkd", value_each, picker_float, precision=lax.Precision.HIGHEST
    ).reshape(local_prompts, suffix_count, KVH * HD)
    key_grad, value_grad = (
        lax.psum_scatter(key_slots, "tensor", scatter_dimension=2, tiled=True),
        lax.psum_scatter(value_slots, "tensor", scatter_dimension=2, tiled=True),
    )
    key_grad = key_grad.astype(jnp.bfloat16)
    value_grad = value_grad.astype(jnp.bfloat16)
    branch = jnp.einsum("pnc,dc->pnd", query_grad, query_full, preferred_element_type=jnp.float32)
    branch = branch + jnp.einsum(
        "pnc,dc->pnd", key_grad, key_full, preferred_element_type=jnp.float32
    )
    branch = branch + jnp.einsum(
        "pnc,dc->pnd", value_grad, value_full, preferred_element_type=jnp.float32
    )
    embed_rows = jnp.einsum("pns,psd->pnd", chooser, embeds, preferred_element_type=jnp.float32)
    norm_rows = lax.rsqrt(jnp.mean(embed_rows * embed_rows, axis=-1, keepdims=True) + EPSILON)
    scaled = embed_rows * norm_rows
    inner = jnp.sum(branch * gain_float * scaled, axis=-1, keepdims=True)
    spread = jnp.broadcast_to(inner, (local_prompts, suffix_count, n_tensor))
    share, inner_total = (
        lax.psum_scatter(branch, "tensor", scatter_dimension=2, tiled=True),
        lax.psum_scatter(spread, "tensor", scatter_dimension=2, tiled=True),
    )
    slice_width = width // n_tensor
    slice_start = lax.axis_index("tensor") * slice_width
    gain_slice = lax.dynamic_slice_in_dim(gain_float, slice_start, slice_width, 0)
    scaled_slice = lax.dynamic_slice_in_dim(scaled, slice_start, slice_width, 2)
    weighted = share * gain_slice
    suffix_grad = (norm_rows * (weighted - scaled_slice * (inner_total / width))).astype(
        jnp.bfloat16
    )
    pieces = lax.all_gather(suffix_grad, ("prompt", "tensor"), axis=0, tiled=True)
    n_prompt = lax.axis_size("prompt")
    pieces = pieces.reshape(n_prompt, n_tensor, local_prompts, suffix_count, slice_width)
    flat_grads = pieces.transpose(0, 2, 3, 1, 4).reshape(-1, width)
    scores = -jnp.einsum("rd,vd->rv", flat_grads, vocab_table, preferred_element_type=jnp.float32)
    scores = scores.reshape(-1, suffix_count, vocab_table.shape[0])
    return jnp.where(banned[None, None, :] == 1, 0.0, scores)


def solution(mesh):
    return jax.shard_map(
        on_device,
        mesh=mesh,
        in_specs=(
            P("prompt", None, "tensor"),
            P(),
            P("prompt", "tensor"),
            P("prompt", "tensor"),
            P("prompt", "tensor"),
            P("tensor", "prompt"),
            P("prompt", None, "tensor"),
            P("prompt", None),
            P(("prompt", "tensor"), None),
            P(("prompt", "tensor")),
        ),
        out_specs=P(None, None, ("prompt", "tensor")),
        check_vma=False,
    )
```

profile of v0, /device:TPU:0, one launch (start us, length us, event | category | flops | bytes accessed | tf_op | source)
XLA Modules:
  0.0 950.5 jit_solution(13312096327044109520)
XLA Ops:
  10.7 24.8 %all-gather.10.cloned.1.call-done = bf16[1,64,8192]{2,1,0:T(8,128)(2,1)} async-done(((bf16[1,64,1024]{2,1,0:T(8,128)(2,1)}), bf16[1,64,8192]{2,1,0:T(8,128)(2,1)}) %all-gather.10.cloned.1.call-update) | async-done | bytes 1048592 | tf_op jit(solution)/shard_map/all_gather | solution.py:36
  38.8 44.2 %all-gather.20.cloned.1.call-done = bf16[8192,128]{1,0:T(8,128)(2,1)} async-done(((bf16[2048,128]{1,0:T(8,128)(2,1)}), bf16[8192,128]{1,0:T(8,128)(2,1)}) %all-gather.20.cloned.1.call-update) | async-done | bytes 2097168 | tf_op jit(solution)/shard_map/all_gather | solution.py:32
  85.1 9.1 all-gather.1
  94.2 35.1 %all-gather.12.cloned.1.call-done = bf16[8192,128]{1,0:T(8,128)(2,1)} async-done(((bf16[2048,128]{1,0:T(8,128)(2,1)}), bf16[8192,128]{1,0:T(8,128)(2,1)}) %all-gather.12.cloned.1.call-update) | async-done | bytes 2097168 | tf_op jit(solution)/shard_map/all_gather | solution.py:31
  131.4 9.2 all-gather
  141.1 12.2 %all-gather.16.cloned.1.call-done = bf16[1,64,8192]{2,1,0:T(8,128)(2,1)} async-done(((bf16[1,64,1024]{2,1,0:T(8,128)(2,1)}), bf16[1,64,8192]{2,1,0:T(8,128)(2,1)}) %all-gather.16.cloned.1.call-update) | async-done | bytes 1048592 | tf_op jit(solution)/shard_map/all_gather | solution.py:37
  153.3 288.2 %all-gather.18.cloned.1.call-done = bf16[1024,8192]{1,0:T(8,128)(2,1)} async-done(((bf16[1024,2048]{1,0:T(8,128)(2,1)}), bf16[1024,8192]{1,0:T(8,128)(2,1)}) %all-gather.18.cloned.1.call-update) | async-done | bytes 16777232 | tf_op jit(solution)/shard_map/all_gather | solution.py:33
  441.5 11.3 %fusion.14 = bf16[8,8,8,128]{3,2,1,0:T(8,128)(2,1)S(1)} fusion(bf16[1024,8192]{1,0:T(8,128)(2,1)} %all-gather.18.cloned.1.call-done, bf16[1,64,8192]{2,1,0:T(8,128)(2,1)} %all-gather.16.cloned.1.call-done), kind=kOutput, calls=%fused_computation.28 | convolution fusion | flops 1073807360 | bytes 17956864 | tf_op jit(solution)/shard_map/psd,cd->psc/dot_general | solution.py:91
  453.0 274.9 %all-gather.14.cloned.1.call-done = bf16[8192,1024]{1,0:T(8,128)(2,1)} async-done(((bf16[2048,1024]{1,0:T(8,128)(2,1)}), bf16[8192,1024]{1,0:T(8,128)(2,1)}) %all-gather.14.cloned.1.call-update) | async-done | bytes 16777232 | tf_op jit(solution)/shard_map/all_gather | solution.py:30
  727.9 8.9 fusion.13
  738.0 7.1 copy.86
  745.1 8.7 bitcast_reduce_fusion.1
  754.3 7.1 copy.88
  761.4 8.9 bitcast_reduce_fusion
  770.8 10.3 %fusion.107 = f32[20,8192]{1,0:T(8,128)S(1)} fusion(bf16[20,1024]{1,0:T(8,128)(2,1)S(1)} %bitcast.181, bf16[8192,1024]{1,0:T(8,128)(2,1)} %all-gather.14.cloned.1.call-done), kind=kOutput, calls=%fused_computation.115 | convolution fusion | flops 335544320 | bytes 17473536 | tf_op jit(solution)/shard_map/pnc,dc->pnd/dot_general | solution.py:136
  781.1 5.2 reduce-scatter.11.cloned.1.call-done
  788.1 35.8 %reduce-scatter.13.cloned.1.call-done = f32[128,20]{1,0:T(8,128)} async-done(((f32[1024,20]{1,0:T(8,128)}), f32[128,20]{1,0:T(8,128)}) %reduce-scatter.13.cloned.1.call-update) | async-done | bytes 10256
  825.8 2.9 convolution_add_fusion.1
  828.7 2.2 multiply_reduce_fusion
  831.7 12.4 %all-reduce = f32[1,20,8]{1,2,0:T(8,128)S(1)} all-reduce(f32[1,20,8]{1,2,0:T(8,128)S(1)} %broadcast_in_dim.49), channel_id=7, replica_groups=mesh['prompt'=4,'tensor'=8] {'tensor'}, use_global_device_ids=true, to_apply=%region_9.10.clone | all-reduce | flops 160 | bytes 1280
  844.8 21.3 %reduce-scatter.9.cloned.1.call-done = f32[1,20,1024]{2,1,0:T(8,128)} async-done(((f32[1,20,8192]{2,1,0:T(8,128)}), f32[1,20,1024]{2,1,0:T(8,128)}) %reduce-scatter.9.cloned.1.call-update) | async-done | bytes 81936 | tf_op jit(solution)/shard_map/reduce_scatter | solution.py:149
  867.7 56.1 %all-gather.22.cloned.1.call-done = bf16[32,20,1024]{2,1,0:T(8,128)(2,1)} async-done(((bf16[1,20,1024]{2,1,0:T(8,128)(2,1)}), bf16[32,20,1024]{2,1,0:T(8,128)(2,1)}) %all-gather.22.cloned.1.call-update) | async-done | bytes 1310736 | tf_op jit(solution)/shard_map/all_gather | solution.py:160
  923.8 2.1 copy.77
  926.7 15.5 %convolution_negate_fusion = f32[80,2048]{1,0:T(8,128)S(1)} fusion(bf16[80,8192]{1,0:T(8,128)(2,1)S(1)} %bitcast.171, bf16[2048,8192]{1,0:T(8,128)(2,1)} %param.18), kind=kOutput, calls=%fused_computation.8 | convolution fusion | flops 2684518400 | bytes 35520512 | tf_op jit(solution)/shard_map/rd,vd->rv/dot_general | solution.py:164
  (70 shorter events, 22.9 us)
Async XLA Ops:
  6.5 29.0 %all-gather.10.cloned.1.call-start = ((), (), s32[]{:S(2)}) async-start(), calls=%async_computation.3 | async-start | bytes 1179648 | tf_op jit(solution)/shard_map/all_gather | solution.py:36
  7.3 75.7 %all-gather.20.cloned.1.call-start = ((), (), s32[]{:S(2)}) async-start(), calls=%async_computation.8 | async-start | bytes 2621440 | tf_op jit(solution)/shard_map/all_gather | solution.py:32
  8.0 121.3 %all-gather.12.cloned.1.call-start = ((), (), s32[]{:S(2)}) async-start(), calls=%async_computation.4 | async-start | bytes 2621440 | tf_op jit(solution)/shard_map/all_gather | solution.py:31
  8.7 144.6 %all-gather.16.cloned.1.call-start = ((), (), s32[]{:S(2)}) async-start(), calls=%async_computation.6 | async-start | bytes 1179648 | tf_op jit(solution)/shard_map/all_gather | solution.py:37
  9.3 432.2 %all-gather.18.cloned.1.call-start = ((), (), s32[]{:S(2)}) async-start(), calls=%async_computation.7 | async-start | bytes 20971520 | tf_op jit(solution)/shard_map/all_gather | solution.py:33
  9.9 0.7 copy-start.2
  9.9 27.2 %copy-start.4 = (s32[1,20]{1,0:T(1,128)S(1)}, s32[1,20]{1,0:T(1,128)}, u32[]{:S(2)}) copy-start(s32[1,20]{1,0:T(1,128)} %param.17) | copy-start | bytes 244
  9.9 718.0 %all-gather.14.cloned.1.call-start = ((), (), s32[]{:S(2)}) async-start(), calls=%async_computation.5 | async-start | bytes 20971520 | tf_op jit(solution)/shard_map/all_gather | solution.py:30
  10.5 775.8 %reduce-scatter.11.cloned.1.call-start = ((), (), s32[]{:S(2)}) async-start(), calls=%async_computation.11 | async-start | bytes 589824
  35.5 47.5 %copy-start = (bf16[1,64,8192]{2,1,0:T(8,128)(2,1)S(1)}, bf16[1,64,8192]{2,1,0:T(8,128)(2,1)}, u32[]{:S(2)}) copy-start(bf16[1,64,8192]{2,1,0:T(8,128)(2,1)} %all-gather.10.cloned.1.call-done) | copy-start | bytes 3145732
  753.8 70.1 %reduce-scatter.13.cloned.1.call-start = ((), (), s32[]{:S(2)}) async-start(), calls=%async_computation.12 | async-start | bytes 589824
  770.7 95.4 %reduce-scatter.9.cloned.1.call-start = ((), (), s32[]{:S(2)}) async-start(), calls=%async_computation.9 | async-start | bytes 884736 | tf_op jit(solution)/shard_map/reduce_scatter | solution.py:149
  825.8 2.9 copy-start.1
  828.7 2.4 copy-start.5
  828.7 39.0 %copy-start.3 = (s32[2048]{0:T(1024)S(1)}, s32[2048]{0:T(1024)}, u32[]{:S(2)}) copy-start(s32[2048]{0:T(1024)} %param.19) | copy-start | bytes 24580
  831.0 92.8 %all-gather.22.cloned.1.call-start = ((), (), s32[]{:S(2)}) async-start(), calls=%async_computation.10 | async-start | bytes 1622016 | tf_op jit(solution)/shard_map/all_gather | solution.py:160
Sparse Core Ops, SparseCore 0:
  9.3 26.1 all-gather.9
  37.1 45.9 all-gather.19
  84.6 44.6 all-gather.11
  131.0 22.1 all-gather.15
  154.7 286.7 all-gather.17
  442.9 284.9 all-gather.13
  754.0 32.3 reduce-scatter.10
  789.7 34.2 reduce-scatter.12
  831.1 34.9 reduce-scatter.8
  868.8 54.9 all-gather.21
where the time goes:
time: 951 us; the launch traced here: 950 us
  waiting for transfers between devices  802 us (84%)
  matrix products  59.2 us (6%)
  local copies, waits for them, and re-layouts  40.5 us (4%)
  blocking collectives  30.7 us (3%)
  between operations  13.8 us (1%)
    all_gather x1, waiting for transfers between devices, on_device(): lax.all_gather(out_weight, 'prompt', axis=1, tiled=True)  288 us
    all_gather x1, waiting for transfers between devices, on_device(): lax.all_gather(query_weight, 'prompt', axis=0, tiled=True)  275 us
    all_gather x1, waiting for transfers between devices, on_device(): lax.all_gather(suffix_grad, ('prompt', 'tensor'), axis=0, tiled=True)  56.1 us
    unnamed x12, waiting for transfers between devices  44.8 us
    all_gather x1, waiting for transfers between devices, on_device(): lax.all_gather(value_weight, 'prompt', axis=0, tiled=True)  44.2 us
    unnamed x24, local copies, waits for them, and re-layouts  36 us
    all_gather x1, waiting for transfers between devices, on_device(): lax.all_gather(key_weight, 'prompt', axis=0, tiled=True)  35.1 us
    all_gather x1, waiting for transfers between devices, on_device(): lax.all_gather(embeds, 'tensor', axis=2, tiled=True)  24.8 us
  transfers between devices with their start and end apart: 10, of which 10 were waited for; matrix products, arithmetic and copies ran while one was open for 5% of the time, Pallas kernels for 0%

commit v1 on v0

v1 whole, which is shorter than its diff:
```python
import math

import jax
import jax.numpy as jnp
from jax import lax
from jax.sharding import PartitionSpec as P

KVH = 8
HD = 128


EPSILON = 1e-05


def dot_f32(spec, a, b):
    return jnp.einsum(spec, a, b, preferred_element_type=jnp.float32)


def on_device(
    embeds,
    norm_gain,
    query_weight,
    key_weight,
    value_weight,
    out_weight,
    out_grad,
    suffix_pos,
    vocab_table,
    banned,
):
    n_prompt = lax.axis_size("prompt")
    n_tensor = lax.axis_size("tensor")
    here_prompt = lax.axis_index("prompt")
    here_tensor = lax.axis_index("tensor")
    seq_len = embeds.shape[1]
    suffix_count = suffix_pos.shape[1]
    width = embeds.shape[2] * n_tensor
    rows_here, head_cols = query_weight.shape
    key_cols = key_weight.shape[1]
    heads_here = head_cols // HD
    slice_width = rows_here // n_tensor
    logit_scale = 1.0 / math.sqrt(HD)

    suffix_all = lax.all_gather(suffix_pos, "prompt", axis=0, tiled=True)
    both = jnp.concatenate([embeds, out_grad], axis=1)
    both = lax.all_gather(both, "tensor", axis=2, tiled=True)
    own = both[:, :seq_len].astype(jnp.float32)
    inverse_norm = lax.rsqrt(jnp.mean(own * own, axis=-1, keepdims=True) + EPSILON)
    inverse_norm = lax.all_gather(inverse_norm, "prompt", axis=0, tiled=True)
    both = lax.all_to_all(both, "prompt", split_axis=2, concat_axis=0, tiled=True)
    embeds = both[:, :seq_len]
    out_grad = both[:, seq_len:]
    embeds_float = embeds.astype(jnp.float32)
    gain_rows = lax.dynamic_slice_in_dim(norm_gain, here_prompt * rows_here, rows_here, 0)
    gain_rows = gain_rows.astype(jnp.float32)
    normed = (embeds_float * inverse_norm * gain_rows).astype(jnp.bfloat16)

    parts = jnp.concatenate(
        [
            dot_f32("psd,dc->psc", normed, query_weight),
            dot_f32("psd,dc->psc", normed, key_weight),
            dot_f32("psd,dc->psc", normed, value_weight),
            dot_f32("psd,cd->psc", out_grad, out_weight),
        ],
        axis=2,
    )
    whole = lax.psum_scatter(parts, "prompt", scatter_dimension=0, tiled=True)
    whole = whole[0].astype(jnp.bfloat16)
    queries = whole[:, :head_cols].reshape(seq_len, heads_here, HD)
    key_values = whole[:, head_cols : head_cols + 2 * key_cols]
    contexts = whole[:, head_cols + 2 * key_cols :].reshape(seq_len, heads_here, HD)
    key_values = lax.all_gather(key_values, "tensor", axis=0, tiled=False)
    key_values = key_values.reshape(n_tensor, seq_len, 2, key_cols).transpose(2, 1, 0, 3)
    key_values = key_values.reshape(2, seq_len, KVH * HD)
    fold = min(heads_here, KVH)
    first = ((here_tensor * heads_here) % KVH) * HD
    if fold < KVH:
        key_values = lax.dynamic_slice_in_dim(key_values, first, fold * HD, 2)
    key_values = key_values.reshape(2, seq_len, fold, HD)
    if heads_here > fold:
        key_values = jnp.tile(key_values, (1, 1, heads_here // fold, 1))
    keys, values = key_values[0], key_values[1]

    logits = dot_f32("qhd,khd->hqk", queries, keys) * logit_scale
    row_index = lax.broadcasted_iota(jnp.int32, (seq_len, seq_len), 0)
    col_index = lax.broadcasted_iota(jnp.int32, (seq_len, seq_len), 1)
    causal = col_index <= row_index
    largest = jnp.max(jnp.where(causal, logits, -1e30), axis=-1, keepdims=True)
    raised = jnp.where(causal, jnp.exp(logits - largest), 0.0)
    probs = raised / jnp.sum(raised, axis=-1, keepdims=True)
    probs_low = probs.astype(jnp.bfloat16)
    prob_grad = dot_f32("qhd,khd->hqk", contexts, values)
    logit_grad = (
        probs * (prob_grad - jnp.sum(prob_grad * probs, axis=-1, keepdims=True)) * logit_scale
    ).astype(jnp.bfloat16)
    steps_iota = lax.broadcasted_iota(jnp.int32, (suffix_count, seq_len), 1)
    chooser = (steps_iota == suffix_pos[0][:, None]).astype(jnp.bfloat16)
    logit_rows = dot_f32("ns,hsk->hnk", chooser, logit_grad).astype(jnp.bfloat16)
    query_grad = dot_f32("hnk,khd->nhd", logit_rows, keys).astype(jnp.bfloat16)
    query_grad = query_grad.reshape(suffix_count, head_cols)
    logit_cols = dot_f32("hqk,nk->hnq", logit_grad, chooser).astype(jnp.bfloat16)
    prob_cols = dot_f32("hqk,nk->hnq", probs_low, chooser).astype(jnp.bfloat16)
    key_each = dot_f32("hnq,qhd->nhd", logit_cols, queries)
    value_each = dot_f32("hnq,qhd->nhd", prob_cols, contexts)
    slots = jnp.stack([key_each, value_each])
    slots = slots.reshape(2, suffix_count, heads_here // fold, fold * HD).sum(axis=2)
    if fold < KVH:
        slots = lax.dynamic_update_slice_in_dim(
            jnp.zeros((2, suffix_count, KVH * HD), jnp.float32), slots, first, 2
        )
    grads = lax.psum_scatter(slots, "tensor", scatter_dimension=2, tiled=True)
    grads = grads.astype(jnp.bfloat16)
    grads = jnp.concatenate([query_grad, grads[0], grads[1]], axis=1)
    grads = lax.all_gather(grads, "prompt", axis=0, tiled=True)
    branch = dot_f32("nc,dc->nd", grads[:, :head_cols], query_weight)
    branch = branch + dot_f32("nc,dc->nd", grads[:, head_cols : head_cols + key_cols], key_weight)
    branch = branch + dot_f32("nc,dc->nd", grads[:, head_cols + key_cols :], value_weight)
    share = lax.psum_scatter(branch, "tensor", scatter_dimension=1, tiled=True)

    start = here_tensor * slice_width
    embeds_slice = lax.dynamic_slice_in_dim(embeds, start, slice_width, 2)
    steps_iota = lax.broadcasted_iota(jnp.int32, (n_prompt, suffix_count, seq_len), 2)
    chooser_all = steps_iota == suffix_all[:, :, None]
    embed_rows = dot_f32("pns,psd->pnd", chooser_all.astype(jnp.bfloat16), embeds_slice)
    norm_rows = jnp.sum(
        jnp.where(chooser_all, inverse_norm[:, None, :, 0], 0.0), axis=-1, keepdims=True
    )
    scaled = (embed_rows * norm_rows).reshape(n_prompt * suffix_count, slice_width)
    norm_rows = norm_rows.reshape(n_prompt * suffix_count, 1)
    gain_slice = lax.dynamic_slice_in_dim(gain_rows, start, slice_width, 0)
    weighted = share * gain_slice
    inner = jnp.sum(weighted * scaled, axis=-1, keepdims=True)
    inner = lax.psum(inner, ("prompt", "tensor")) / width
    suffix_grad = (norm_rows * (weighted - scaled * inner)).astype(jnp.bfloat16)
    flat_grads = lax.all_gather(suffix_grad, ("prompt", "tensor"), axis=1, tiled=True)
    scores = -dot_f32("rd,vd->rv", flat_grads, vocab_table)
    scores = scores.reshape(n_prompt, suffix_count, vocab_table.shape[0])
    return jnp.where(banned[None, None, :] == 1, 0.0, scores)


def solution(mesh):
    return jax.shard_map(
        on_device,
        mesh=mesh,
        in_specs=(
            P("prompt", None, "tensor"),
            P(),
            P("prompt", "tensor"),
            P("prompt", "tensor"),
            P("prompt", "tensor"),
            P("tensor", "prompt"),
            P("prompt", None, "tensor"),
            P("prompt", None),
            P(("prompt", "tensor"), None),
            P(("prompt", "tensor")),
        ),
        out_specs=P(None, None, ("prompt", "tensor")),
        check_vma=False,
    )
```

time: 951 us -> 441 us (0.46)
  waiting for transfers between devices: 802 us -> 196 us
  blocking collectives: 30.7 us -> 111 us
  other arithmetic: 4.08 us -> 57 us
  matrix products: 59.2 us -> 33.6 us
  local copies, waits for them, and re-layouts: 40.5 us -> 24 us
    all_gather x7 -> x2, waiting for transfers between devices: 736 us -> 86 us  [the longest x1 54.4 us: on_device(): lax.all_gather(suffix_grad, ('prompt', 'tensor'), axis=1, tiled=True)]
    reduce_scatter x1 -> x3, waiting for transfers between devices: 21.3 us -> 101 us  [the longest x1 48.5 us: on_device(): whole = lax.psum_scatter(parts, 'prompt', scatter_dimension=0, tiled=True)]
    unnamed x0 -> x3, other arithmetic: none -> 45.3 us
    unnamed x12 -> x5, waiting for transfers between devices: 44.8 us -> 0.08 us
    psum x0 -> x1, blocking collectives: none -> 39.4 us  [on_device(): inner = lax.psum(inner, ('prompt', 'tensor')) / width]
    unnamed x24 -> x28, local copies, waits for them, and re-layouts: 36 us -> 9.94 us
    dot_general x18 -> x14, matrix products: 59.2 us -> 33.6 us  [dot_f32(): return jnp.einsum(spec, a, b, preferred_element_type=jnp.float32)]
    unnamed x1, blocking collectives: 12.4 us -> 36.9 us
  transfers between devices with their start and end apart: 10 -> 6, of which waited for: 10 -> 6; matrix products, arithmetic and copies ran while one was open for 5% -> 1% of each run, Pallas kernels for 0% -> 0%
where the time goes in v1:
time: 441 us; the launch traced here: 440 us
  waiting for transfers between devices  196 us (44%)
  blocking collectives  111 us (25%)
  other arithmetic  57 us (13%)
  matrix products  33.6 us (8%)
  local copies, waits for them, and re-layouts  24 us (5%)
  between operations  14.1 us (3%)
  starting transfers between devices  4.86 us (1%)
    all_gather x1, waiting for transfers between devices, on_device(): lax.all_gather(suffix_grad, ('prompt', 'tensor'), axis=1, tiled=True)  54.4 us
    reduce_scatter x1, waiting for transfers between devices, on_device(): whole = lax.psum_scatter(parts, 'prompt', scatter_dimension=0, tiled=True)  48.5 us
    unnamed x3, other arithmetic  45.3 us
    psum x1, blocking collectives, on_device(): inner = lax.psum(inner, ('prompt', 'tensor')) / width  39.4 us
    unnamed x1, blocking collectives  36.9 us
    dot_general x14, matrix products, dot_f32(): return jnp.einsum(spec, a, b, preferred_element_type=jnp.float32)  33.6 us
    all_gather x1, waiting for transfers between devices, on_device(): both = lax.all_gather(both, 'tensor', axis=2, tiled=True)  31.6 us
    reduce_scatter x1, waiting for transfers between devices, on_device(): grads = lax.psum_scatter(slots, 'tensor', scatter_dimension=2, tiled=True)  29.7 us
  transfers between devices with their start and end apart: 6, of which 6 were waited for; matrix products, arithmetic and copies ran while one was open for 1% of the time, Pallas kernels for 0%

profile of v1, /device:TPU:0, one launch (start us, length us, event | category | flops | bytes accessed | tf_op | source)
XLA Modules:
  0.0 440.1 jit_solution(10545317299658269144)
XLA Ops:
  6.5 1.7 pad_maximum_fusion.1
  8.3 31.6 %all-gather.7.cloned.1.call-done = bf16[1,128,8192]{2,1,0:T(8,128)(2,1)} async-done(((bf16[1,128,1024]{2,1,0:T(8,128)(2,1)}), bf16[1,128,8192]{2,1,0:T(8,128)(2,1)}) %all-gather.7.cloned.1.call-update) | async-done | bytes 2097168 | tf_op jit(solution)/shard_map/all_gather | solution.py:46
  39.9 9.5 %copy.48 = bf16[1,128,8192]{1,0,2:T(2,128)(2,1)} copy(bf16[1,128,8192]{2,1,0:T(8,128)(2,1)} %all-gather.7.cloned.1.call-done) | data formatting | bytes 4194304 | tf_op jit(solution)/shard_map/all_gather | solution.py:46
  49.9 45.2 %reduce.1 = bf16[8192,128]{1,0:T(8,128)(2,1)S(1)} reduce(bf16[8192,1,128]{2,1,0:T(2,128)(2,1)} %bitcast.91, bf16[]{:T(256)} %broadcast.47), dimensions={1}, to_apply=%bitcast.83.reduce_sub_computation | reduce | bytes 4194306
  95.1 2.1 reshape.85
  97.2 4.7 %all-to-all-start = ((bf16[4,2,131072]{2,1,0:T(2,128)(2,1)}), bf16[4,2,131072]{2,1,0:T(2,128)(2,1)S(1)}, u32[]{:S(2)}, u32[]{:S(2)}) async-start(bf16[4,2,131072]{2,1,0:T(2,128)(2,1)} %reshape.85), calls=%async_computation | async-start | bytes 4194304 | tf_op jit(solution)/shard_map/all_to_all | solution.py:50
  105.5 36.9 %all-reduce = f32[256]{0:T(256)S(1)} all-reduce(f32[256]{0:T(256)S(1)} %rsqrt_dynamic-update-slice_fusion), channel_id=2, replica_groups=mesh['prompt'=4,'tensor'=8] {'prompt'}, use_global_device_ids=true, to_apply=%add | all-reduce | flops 256 | bytes 2048
  142.5 8.3 %all-to-all-done = bf16[4,2,131072]{2,1,0:T(2,128)(2,1)S(1)} async-done(((bf16[4,2,131072]{2,1,0:T(2,128)(2,1)}), bf16[4,2,131072]{2,1,0:T(2,128)(2,1)S(1)}, u32[]{:S(2)}, u32[]{:S(2)}) %all-to-all-start) | async-done | bytes 2097184 | tf_op jit(solution)/shard_map/all_to_all | solution.py:50
  150.8 3.4 reshape.86
  154.1 2.5 copy.67
  156.6 2.7 copy.49
  159.3 1.9 fusion.18
  161.8 3.6 fusion.4
  168.4 48.5 %reduce-scatter.4.cloned.1.call-done = f32[1,64,2304]{2,1,0:T(8,128)} async-done(((f32[4,64,2304]{2,1,0:T(8,128)}), f32[1,64,2304]{2,1,0:T(8,128)}) %reduce-scatter.4.cloned.1.call-update) | async-done | bytes 589840 | tf_op jit(solution)/shard_map/reduce_scatter | solution.py:67
  218.1 9.5 %all-gather.1 = bf16[512,256]{1,0:T(8,128)(2,1)S(1)} all-gather(bf16[64,256]{1,0:T(8,128)(2,1)S(1)} %slice.55), channel_id=3, replica_groups=mesh['prompt'=4,'tensor'=8] {'tensor'}, dimensions={0}, use_global_device_ids=true | all-gather | bytes 294912 | tf_op jit(solution)/shard_map/all_gather | solution.py:72
  233.2 1.7 fusion.14
  235.0 29.7 %reduce-scatter.6.cloned.1.call-done = f32[2,20,128]{2,1,0:T(8,128)} async-done(((f32[2,20,1024]{2,1,0:T(8,128)}), f32[2,20,128]{2,1,0:T(8,128)}) %reduce-scatter.6.cloned.1.call-update) | async-done | bytes 20496 | tf_op jit(solution)/shard_map/reduce_scatter | solution.py:111
  265.4 13.9 %all-gather.3 = bf16[4,20,1280]{2,1,0:T(8,128)(2,1)S(1)} all-gather(bf16[1,20,1280]{2,1,0:T(8,128)(2,1)S(1)} %maximum_bitcast_fusion.1), channel_id=1, replica_groups=mesh['prompt'=4,'tensor'=8] {'prompt'}, dimensions={0}, use_global_device_ids=true | all-gather | bytes 256000 | tf_op jit(solution)/shard_map/all_gather | solution.py:114
  280.9 4.4 %fusion.6 = f32[80,2048]{1,0:T(8,128)} fusion(f32[80,2048]{1,0:T(8,128)S(1)} %fusion.49, f32[80,2048]{1,0:T(8,128)S(1)} %fusion.51, bf16[2048,1024]{1,0:T(8,128)(2,1)} %param.12, bf16[80,1280]{1,0:T(8,128)(2,1)S(1)} %reshape.77), kind=kOutput, calls=%fused_computation.7 | convolution fusion | flops 335872000 | bytes 6324224 | tf_op jit(solution)/shard_map/nc,dc->nd/dot_general | solution.py:16
  285.6 11.1 %all-gather.2 = s32[4,1,20]{2,1,0:T(1,128)S(1)} all-gather(s32[1,1,20]{2,1,0:T(1,128)S(1)} %bitcast.112), channel_id=1, replica_groups=mesh['prompt'=4,'tensor'=8] {'prompt'}, dimensions={0}, use_global_device_ids=true | all-gather | bytes 400 | tf_op jit(solution)/shard_map/all_gather | solution.py:44
  297.2 23.2 %reduce-scatter.8.cloned.1.call-done = f32[80,256]{1,0:T(8,128)} async-done(((f32[80,2048]{1,0:T(8,128)}), f32[80,256]{1,0:T(8,128)}) %reduce-scatter.8.cloned.1.call-update) | async-done | bytes 81936 | tf_op jit(solution)/shard_map/reduce_scatter | solution.py:118
  321.5 39.4 %psum.7 = f32[80,1]{0,1:T(1,128)S(1)} all-reduce(f32[80,1]{0,1:T(1,128)S(1)} %bitcast.108), channel_id=1, replica_groups=mesh['prompt'=4,'tensor'=8] {'prompt','tensor'}, use_global_device_ids=true, to_apply=%region_9.10 | all-reduce | flops 80 | bytes 640 | tf_op jit(solution)/shard_map/psum | solution.py:133
  362.5 54.4 %all-gather.9.cloned.1.call-done = bf16[80,8192]{1,0:T(8,128)(2,1)} async-done(((bf16[80,256]{1,0:T(8,128)(2,1)}), bf16[80,8192]{1,0:T(8,128)(2,1)}) %all-gather.9.cloned.1.call-update) | async-done | bytes 1310736 | tf_op jit(solution)/shard_map/all_gather | solution.py:135
  416.9 15.3 %convolution_negate_fusion = f32[80,2048]{1,0:T(8,128)S(1)} fusion(bf16[80,8192]{1,0:T(8,128)(2,1)} %all-gather.9.cloned.1.call-done, bf16[2048,8192]{1,0:T(8,128)(2,1)} %param.18), kind=kOutput, calls=%fused_computation.8 | convolution fusion | flops 2684518400 | bytes 35520512 | tf_op jit(solution)/shard_map/rd,vd->rv/dot_general | solution.py:16
  (76 shorter events, 20.9 us)
Async XLA Ops:
  6.5 152.8 %copy-start = (bf16[2048,128]{1,0:T(8,128)(2,1)S(1)}, bf16[2048,128]{1,0:T(8,128)(2,1)}, u32[]{:S(2)}) copy-start(bf16[2048,128]{1,0:T(8,128)(2,1)} %param.14) | copy-start | bytes 1572868
  6.5 33.4 %all-gather.7.cloned.1.call-start = ((), (), s32[]{:S(2)}) async-start(), calls=%async_computation.4 | async-start | bytes 2359296 | tf_op jit(solution)/shard_map/all_gather | solution.py:46
  97.2 4.7 %copy-start.8 = (u32[32]{0:T(128)S(1)}, u32[32]{0:T(128)}, u32[]{:S(2)}) copy-start(u32[32]{0:T(128)} %constant.38) | copy-start | bytes 388
  97.2 53.6 %all-to-all-start = ((bf16[4,2,131072]{2,1,0:T(2,128)(2,1)}), bf16[4,2,131072]{2,1,0:T(2,128)(2,1)S(1)}, u32[]{:S(2)}, u32[]{:S(2)}) async-start(bf16[4,2,131072]{2,1,0:T(2,128)(2,1)} %reshape.85), calls=%async_computation | async-start | bytes 4194304 | tf_op jit(solution)/shard_map/all_to_all | solution.py:50
  101.9 115.0 %reduce-scatter.4.cloned.1.call-start = ((), (), s32[]{:S(2)}) async-start(), calls=%async_computation.5 | async-start | bytes 2949120 | tf_op jit(solution)/shard_map/reduce_scatter | solution.py:67
  159.3 1.9 copy-start.1
  159.3 2.0 copy-start.2
  161.8 3.7 copy-start.7
  168.4 96.2 %reduce-scatter.6.cloned.1.call-start = ((), (), s32[]{:S(2)}) async-start(), calls=%async_computation.6 | async-start | bytes 221184 | tf_op jit(solution)/shard_map/reduce_scatter | solution.py:111
  168.4 61.2 %copy-start.6 = (s32[1,20]{1,0:T(1,128)S(1)}, s32[1,20]{1,0:T(1,128)}, u32[]{:S(2)}) copy-start(s32[1,20]{1,0:T(1,128)} %param.17) | copy-start | bytes 244
  227.9 3.1 copy-start.3
  228.1 0.7 copy-start.4
  233.2 87.3 %reduce-scatter.8.cloned.1.call-start = ((), (), s32[]{:S(2)}) async-start(), calls=%async_computation.7 | async-start | bytes 737280 | tf_op jit(solution)/shard_map/reduce_scatter | solution.py:118
  285.4 77.1 %copy-start.5 = (s32[2048]{0:T(1024)S(1)}, s32[2048]{0:T(1024)}, u32[]{:S(2)}) copy-start(s32[2048]{0:T(1024)} %param.19) | copy-start | bytes 24580
  285.4 131.5 %all-gather.9.cloned.1.call-start = ((), (), s32[]{:S(2)}) async-start(), calls=%async_computation.8 | async-start | bytes 1351680 | tf_op jit(solution)/shard_map/all_gather | solution.py:135
Sparse Core Ops, SparseCore 0:
  9.3 30.5 all-gather.6
  168.5 48.4 reduce-scatter.3
  233.3 31.2 reduce-scatter.5
  285.5 34.8 reduce-scatter.7
  362.6 54.2 all-gather.8

commit v2 on v1

--- a/solution.py
+++ b/solution.py
@@ -1,8 +1,11 @@
+import functools
 import math
 
 import jax
 import jax.numpy as jnp
 from jax import lax
+from jax.experimental import pallas as pl
+from jax.experimental.pallas import tpu as pltpu
 from jax.sharding import PartitionSpec as P
 
 KVH = 8
@@ -10,6 +13,67 @@
 
 
 EPSILON = 1e-05
+
+
+def exchange_kernel(axis, count, spread, *refs):
+    arrays = len(spread)
+    sources, targets = refs[:arrays], refs[arrays : 2 * arrays]
+    send_sem, recv_sem, own_sem = refs[2 * arrays :]
+    here = lax.axis_index(axis)
+
+    def block(i, to):
+        return sources[i].at[to] if spread[i] else sources[i]
+
+    kept = []
+    for i in range(arrays):
+        copy = pltpu.make_async_copy(block(i, here), targets[i].at[here], own_sem.at[i])
+        copy.start()
+        kept.append(copy)
+    barrier = pltpu.get_barrier_semaphore()
+    for step in range(1, count):
+        peer = lax.rem(here + step, count)
+        pl.semaphore_signal(
+            barrier, inc=1, device_id={axis: peer}, device_id_type=pl.DeviceIdType.MESH
+        )
+    pl.semaphore_wait(barrier, count - 1)
+    copies = []
+    for step in range(1, count):
+        peer = lax.rem(here + step, count)
+        for i in range(arrays):
+            copy = pltpu.make_async_remote_copy(
+                src_ref=block(i, peer),
+                dst_ref=targets[i].at[here],
+                send_sem=send_sem.at[i, step - 1],
+                recv_sem=recv_sem.at[i, step - 1],
+                device_id={axis: peer},
+                device_id_type=pl.DeviceIdType.MESH,
+            )
+            copy.start()
+            copies.append(copy)
+    for copy in kept + copies:
+        copy.wait()
+
+
+def exchange(axis, number, *operands):
+    count = lax.axis_size(axis)
+    arrays = [array for array, _ in operands]
+    spread = tuple(each for _, each in operands)
+    shapes = [
+        jax.ShapeDtypeStruct(((count,) + (a.shape[1:] if each else a.shape)), a.dtype)
+        for a, each in operands
+    ]
+    space = pl.BlockSpec(memory_space=pltpu.VMEM)
+    sems = pltpu.SemaphoreType.DMA((len(arrays), count - 1))
+    return pl.pallas_call(
+        functools.partial(exchange_kernel, axis, count, spread),
+        out_shape=shapes,
+        in_specs=[space] * len(arrays),
+        out_specs=[space] * len(arrays),
+        scratch_shapes=[sems, sems, pltpu.SemaphoreType.DMA((len(arrays),))],
+        compiler_params=pltpu.CompilerParams(
+            collective_id=number, has_side_effects=True, vmem_limit_bytes=40 << 20
+        ),
+    )(*arrays)
 
 
 def dot_f32(spec, a, b):
@@ -41,15 +105,30 @@
     slice_width = rows_here // n_tensor
     logit_scale = 1.0 / math.sqrt(HD)
 
-    suffix_all = lax.all_gather(suffix_pos, "prompt", axis=0, tiled=True)
-    both = jnp.concatenate([embeds, out_grad], axis=1)
-    both = lax.all_gather(both, "tensor", axis=2, tiled=True)
-    own = both[:, :seq_len].astype(jnp.float32)
-    inverse_norm = lax.rsqrt(jnp.mean(own * own, axis=-1, keepdims=True) + EPSILON)
-    inverse_norm = lax.all_gather(inverse_norm, "prompt", axis=0, tiled=True)
-    both = lax.all_to_all(both, "prompt", split_axis=2, concat_axis=0, tiled=True)
-    embeds = both[:, :seq_len]
-    out_grad = both[:, seq_len:]
+    split_rows = seq_len // n_tensor
+    ratio = n_tensor // n_prompt
+    feature_cols = embeds.shape[2]
+    both = jnp.concatenate(
+        [
+            embeds.reshape(n_tensor, split_rows, feature_cols),
+            out_grad.reshape(n_tensor, split_rows, feature_cols),
+        ],
+        axis=1,
+    )
+    (both,) = exchange("tensor", 0, (both, True))
+    own = both[:, :split_rows].astype(jnp.float32)
+    inverse_norm = lax.rsqrt(jnp.sum(own * own, axis=(0, 2))[:, None] / width + EPSILON)
+    inverse_norm = jnp.broadcast_to(inverse_norm, (split_rows, 128))
+    both = both.reshape(n_prompt, ratio, 2 * split_rows, feature_cols)
+    both, inverse_norm, suffix_all = exchange(
+        "prompt", 1, (both, True), (inverse_norm, False), (suffix_pos, False)
+    )
+    both, inverse_norm = exchange("tensor", 2, (both, False), (inverse_norm, False))
+    suffix_all = suffix_all.reshape(n_prompt, suffix_count)
+    both = both.reshape(n_tensor, n_prompt, ratio, 2, split_rows, feature_cols)
+    both = both.transpose(3, 1, 0, 4, 2, 5).reshape(2, n_prompt, seq_len, rows_here)
+    embeds, out_grad = both[0], both[1]
+    inverse_norm = inverse_norm[..., :1].transpose(1, 0, 2, 3).reshape(n_prompt, seq_len, 1)
     embeds_float = embeds.astype(jnp.float32)
     gain_rows = lax.dynamic_slice_in_dim(norm_gain, here_prompt * rows_here, rows_here, 0)
     gain_rows = gain_rows.astype(jnp.float32)
@@ -60,16 +139,16 @@
             dot_f32("psd,dc->psc", normed, query_weight),
             dot_f32("psd,dc->psc", normed, key_weight),
             dot_f32("psd,dc->psc", normed, value_weight),
-            dot_f32("psd,cd->psc", out_grad, out_weight),
         ],
         axis=2,
     )
-    whole = lax.psum_scatter(parts, "prompt", scatter_dimension=0, tiled=True)
-    whole = whole[0].astype(jnp.bfloat16)
+    context_parts = dot_f32("psd,cd->psc", out_grad, out_weight).astype(jnp.bfloat16)
+    parts, context_parts = exchange("prompt", 3, (parts, True), (context_parts, True))
+    whole = jnp.sum(parts, axis=0).astype(jnp.bfloat16)
+    contexts = jnp.sum(context_parts.astype(jnp.float32), axis=0).astype(jnp.bfloat16)
+    contexts = contexts.reshape(seq_len, heads_here, HD)
     queries = whole[:, :head_cols].reshape(seq_len, heads_here, HD)
-    key_values = whole[:, head_cols : head_cols + 2 * key_cols]
-    contexts = whole[:, head_cols + 2 * key_cols :].reshape(seq_len, heads_here, HD)
-    key_values = lax.all_gather(key_values, "tensor", axis=0, tiled=False)
+    (key_values,) = exchange("tensor", 4, (whole[:, head_cols:], False))
     key_values = key_values.reshape(n_tensor, seq_len, 2, key_cols).transpose(2, 1, 0, 3)
     key_values = key_values.reshape(2, seq_len, KVH * HD)
     fold = min(heads_here, KVH)
@@ -108,31 +187,36 @@
         slots = lax.dynamic_update_slice_in_dim(
             jnp.zeros((2, suffix_count, KVH * HD), jnp.float32), slots, first, 2
         )
-    grads = lax.psum_scatter(slots, "tensor", scatter_dimension=2, tiled=True)
-    grads = grads.astype(jnp.bfloat16)
+    slots = slots.reshape(2 * suffix_count, n_tensor, key_cols).transpose(1, 0, 2)
+    (grads,) = exchange("tensor", 5, (slots, True))
+    grads = jnp.sum(grads, axis=0).astype(jnp.bfloat16).reshape(2, suffix_count, key_cols)
     grads = jnp.concatenate([query_grad, grads[0], grads[1]], axis=1)
-    grads = lax.all_gather(grads, "prompt", axis=0, tiled=True)
+    (grads,) = exchange("prompt", 6, (grads, False))
+    rows = n_prompt * suffix_count
+    grads = grads.reshape(rows, head_cols + 2 * key_cols)
+    steps_iota = lax.broadcasted_iota(jnp.int32, (n_prompt, suffix_count, seq_len), 2)
+    chooser_all = steps_iota == suffix_all[:, :, None]
+    embed_rows = dot_f32("pns,psd->pnd", chooser_all.astype(jnp.bfloat16), embeds)
+    norm_rows = jnp.sum(
+        jnp.where(chooser_all, inverse_norm[:, None, :, 0], 0.0), axis=-1, keepdims=True
+    )
+    scaled = (embed_rows * norm_rows).reshape(rows, rows_here)
+    norm_rows = norm_rows.reshape(rows, 1)
     branch = dot_f32("nc,dc->nd", grads[:, :head_cols], query_weight)
     branch = branch + dot_f32("nc,dc->nd", grads[:, head_cols : head_cols + key_cols], key_weight)
     branch = branch + dot_f32("nc,dc->nd", grads[:, head_cols + key_cols :], value_weight)
-    share = lax.psum_scatter(branch, "tensor", scatter_dimension=1, tiled=True)
-
-    start = here_tensor * slice_width
-    embeds_slice = lax.dynamic_slice_in_dim(embeds, start, slice_width, 2)
-    steps_iota = lax.broadcasted_iota(jnp.int32, (n_prompt, suffix_count, seq_len), 2)
-    chooser_all = steps_iota == suffix_all[:, :, None]
-    embed_rows = dot_f32("pns,psd->pnd", chooser_all.astype(jnp.bfloat16), embeds_slice)
-    norm_rows = jnp.sum(
-        jnp.where(chooser_all, inverse_norm[:, None, :, 0], 0.0), axis=-1, keepdims=True
-    )
-    scaled = (embed_rows * norm_rows).reshape(n_prompt * suffix_count, slice_width)
-    norm_rows = norm_rows.reshape(n_prompt * suffix_count, 1)
-    gain_slice = lax.dynamic_slice_in_dim(gain_rows, start, slice_width, 0)
-    weighted = share * gain_slice
-    inner = jnp.sum(weighted * scaled, axis=-1, keepdims=True)
-    inner = lax.psum(inner, ("prompt", "tensor")) / width
+    branch = branch * gain_rows
+    inner = jnp.sum(branch * scaled, axis=-1)
+    branch = branch.reshape(rows, n_tensor, slice_width).transpose(1, 0, 2)
+    share, inner = exchange("tensor", 7, (branch, True), (inner[None, :], False))
+    weighted = jnp.sum(share, axis=0)
+    (inner,) = exchange("prompt", 8, (jnp.sum(inner, axis=0), False))
+    inner = jnp.sum(inner, axis=0).reshape(rows, 1) / width
+    scaled = lax.dynamic_slice_in_dim(scaled, here_tensor * slice_width, slice_width, 1)
     suffix_grad = (norm_rows * (weighted - scaled * inner)).astype(jnp.bfloat16)
-    flat_grads = lax.all_gather(suffix_grad, ("prompt", "tensor"), axis=1, tiled=True)
+    (suffix_grad,) = exchange("prompt", 9, (suffix_grad, False))
+    (suffix_grad,) = exchange("tensor", 10, (suffix_grad, False))
+    flat_grads = suffix_grad.transpose(2, 1, 0, 3).reshape(rows, width)
     scores = -dot_f32("rd,vd->rv", flat_grads, vocab_table)
     scores = scores.reshape(n_prompt, suffix_count, vocab_table.shape[0])
     return jnp.where(banned[None, None, :] == 1, 0.0, scores)

time: 441 us -> 188 us (0.43)
  waiting for transfers between devices: 196 us -> 0 us
  Pallas kernels: 0 us -> 149 us
  blocking collectives: 111 us -> 0 us
  other arithmetic: 57 us -> 2.83 us
  local copies, waits for them, and re-layouts: 24 us -> 8.87 us
  between operations: 14.1 us -> 0.48 us
  matrix products: 33.6 us -> 25.2 us
  starting transfers between devices: 4.86 us -> 0 us
    pallas_call x0 -> x11, Pallas kernels: none -> 149 us  [exchange(): pl.pallas_call(functools.partial(exchange_kernel, axis, count, spread), o...]
    reduce_scatter x3 -> x0, waiting for transfers between devices: 101 us -> none  [the longest x1 48.5 us: on_device(): whole = lax.psum_scatter(parts, 'prompt', scatter_dimension=0, tiled=True)]
    all_gather x2 -> x0, waiting for transfers between devices: 86 us -> none  [the longest x1 54.4 us: on_device(): lax.all_gather(suffix_grad, ('prompt', 'tensor'), axis=1, tiled=True)]
    unnamed x3 -> x0, other arithmetic: 45.3 us -> none
    psum x1 -> x0, blocking collectives: 39.4 us -> none  [on_device(): inner = lax.psum(inner, ('prompt', 'tensor')) / width]
    unnamed x1 -> x0, blocking collectives: 36.9 us -> none
    all_gather x3 -> x0, blocking collectives: 34.5 us -> none  [the longest x1 13.9 us: on_device(): grads = lax.all_gather(grads, 'prompt', axis=0, tiled=True)]
    all_gather x1 -> x0, local copies, waits for them, and re-layouts: 9.49 us -> none  [on_device(): both = lax.all_gather(both, 'tensor', axis=2, tiled=True)]
  transfers between devices with their start and end apart: 6 -> 0, of which waited for: 6 -> 0; matrix products, arithmetic and copies ran while one was open for 1% -> 0% of each run, Pallas kernels for 0% -> 0%
where the time goes in v2:
time: 188 us; the launch traced here: 187 us
  Pallas kernels  149 us (79%)
  matrix products  25.2 us (13%)
  local copies, waits for them, and re-layouts  8.87 us (5%)
  other arithmetic  2.83 us (2%)
    pallas_call x11, Pallas kernels, exchange(): pl.pallas_call(functools.partial(exchange_kernel, axis, count, spread), o...  149 us
    dot_general x14, matrix products, dot_f32(): return jnp.einsum(spec, a, b, preferred_element_type=jnp.float32)  25.2 us
    unnamed x21, local copies, waits for them, and re-layouts  4.72 us

profile of v2, /device:TPU:0, one launch (start us, length us, event | category | flops | bytes accessed | tf_op | source)
XLA Modules:
  0.0 186.9 jit_solution(2267377002972848125)
XLA Ops:
  0.0 1.0 pad_maximum_fusion.1.refs_0_
  1.0 8.1 %shard_map.100 = bf16[8,16,1024]{2,1,0:T(8,128)(2,1)S(1)} custom-call(bf16[8,16,1024]{2,1,0:T(8,128)(2,1)S(1)} %pad_maximum_fusion.1.refs_0_), custom_call_target="tpu_custom_call" | custom-call | tf_op jit(solution)/shard_map/pallas_call | solution.py:67
  9.5 0.7 copy-done.2
  10.1 9.7 %shard_map.101 = (bf16[4,2,16,1024]{3,2,1,0:T(8,128)(2,1)S(1)}, f32[4,8,128]{2,1,0:T(8,128)S(1)}, s32[4,1,20]{2,1,0:T(1,128)S(1)}) custom-call(bf16[4,2,16,1024]{3,2,1,0:T(8,128)(2,1)S(1)} %bitcast.120, f32[8,128]{1,0:T(8,128)S(1)} %broadcast_in_dim.58.refs_1_, s32[1,20]{1,0:T(1,128)S(1)} %copy-done.2), custom_call_target="tpu_custom_call" | custom-call | tf_op jit(solution)/shard_map/pallas_call | solution.py:67
  19.8 27.1 %shard_map.102 = (bf16[8,4,2,16,1024]{4,3,2,1,0:T(8,128)(2,1)S(1)}, f32[8,4,8,128]{3,2,1,0:T(8,128)S(1)}) custom-call(bf16[4,2,16,1024]{3,2,1,0:T(8,128)(2,1)S(1)} %get-tuple-element.15.refs_0_, f32[4,8,128]{2,1,0:T(8,128)S(1)} %get-tuple-element.16.refs_1_), custom_call_target="tpu_custom_call" | custom-call | tf_op jit(solution)/shard_map/pallas_call | solution.py:67
  48.1 0.9 reshape.101
  49.0 0.7 dynamic-slice_convert_fusion
  50.8 1.2 copy-done.4
  52.0 1.3 fusion.4
  53.5 2.0 %copy-done.8 = bf16[1024,2048]{1,0:T(8,128)(2,1)S(1)} copy-done((bf16[1024,2048]{1,0:T(8,128)(2,1)S(1)}, bf16[1024,2048]{1,0:T(8,128)(2,1)}, u32[]{:S(2)}) %copy-start.8) | copy-done | bytes 4194328
  55.5 1.3 fusion.8.refs_1_
  56.8 35.8 %shard_map.103 = (f32[4,64,1280]{2,1,0:T(8,128)S(1)}, bf16[4,64,1024]{2,1,0:T(8,128)(2,1)S(1)}) custom-call(f32[4,64,1280]{2,1,0:T(8,128)S(1)} %pad_maximum_fusion.refs_0_, bf16[4,64,1024]{2,1,0:T(8,128)(2,1)S(1)} %fusion.8.refs_1_), custom_call_target="tpu_custom_call" | custom-call | tf_op jit(solution)/shard_map/pallas_call | solution.py:67
  92.7 5.7 %shard_map.104 = bf16[8,64,256]{2,1,0:T(8,128)(2,1)S(1)} custom-call(bf16[64,256]{1,0:T(8,128)(2,1)S(1)} %slice.58.refs_0_), custom_call_target="tpu_custom_call" | custom-call | tf_op jit(solution)/shard_map/pallas_call | solution.py:67
  100.0 5.7 %shard_map.105 = f32[8,40,128]{2,1,0:T(8,128)S(1)} custom-call(f32[8,40,128]{2,1,0:T(8,128)S(1)} %bitcast.121), custom_call_target="tpu_custom_call" | custom-call | tf_op jit(solution)/shard_map/pallas_call | solution.py:67
  106.2 17.6 %shard_map.106 = bf16[4,20,1280]{2,1,0:T(8,128)(2,1)S(1)} custom-call(bf16[20,1280]{1,0:T(8,128)(2,1)S(1)} %pad_maximum_fusion.3.refs_0_), custom_call_target="tpu_custom_call" | custom-call | tf_op jit(solution)/shard_map/pallas_call | solution.py:67
  124.5 3.7 %multiply_reduce_fusion = (f32[80]{0:T(128)S(1)}, f32[80,2048]{1,0:T(8,128)S(1)}) fusion(f32[80,2048]{1,0:T(8,128)S(1)} %copy-done.5, f32[2048]{0:T(1024)S(1)} %dynamic-slice_convert_fusion, f32[80,2048]{1,0:T(8,128)S(1)} %fusion.51, f32[80,2048]{1,0:T(8,128)S(1)} %fusion.53, bf16[2048,1024]{1,0:T(8,128)(2,1)} %param.12, bf16[80,1280]{1,0:T(8,128)(2,1)S(1)} %reshape.99), kind=kOutput, calls=%fused_computation.32 | convolution fusion | flops 336363456 | bytes 6988096 | tf_op jit(solution)/shard_map/nc,dc->nd/dot_general | solution.py:80
  128.3 9.8 %shard_map.107 = (f32[8,80,256]{2,1,0:T(8,128)S(1)}, f32[8,1,80]{2,1,0:T(1,128)S(1)}) custom-call(f32[8,80,256]{2,1,0:T(8,128)S(1)} %bitcast.118, f32[1,80]{1,0:T(1,128)S(1)} %bitcast.125), custom_call_target="tpu_custom_call" | custom-call | tf_op jit(solution)/shard_map/pallas_call | solution.py:67
  138.2 5.9 %shard_map.108 = f32[4,1,80]{2,1,0:T(1,128)S(1)} custom-call(f32[1,80]{1,0:T(1,128)S(1)} %bitcast.124), custom_call_target="tpu_custom_call" | custom-call | tf_op jit(solution)/shard_map/pallas_call | solution.py:67
  144.3 7.5 %shard_map.109.refs_0_ = bf16[4,80,256]{2,1,0:T(8,128)(2,1)S(1)} custom-call(bf16[80,256]{1,0:T(8,128)(2,1)S(1)} %multiply_convert_fusion.4.refs_0_), custom_call_target="tpu_custom_call" | custom-call | tf_op jit(solution)/shard_map/pallas_call | solution.py:67
  151.8 16.5 %shard_map.110 = bf16[8,4,80,256]{3,2,1,0:T(8,128)(2,1)S(1)} custom-call(bf16[4,80,256]{2,1,0:T(8,128)(2,1)S(1)} %shard_map.109.refs_0_), custom_call_target="tpu_custom_call" | custom-call | tf_op jit(solution)/shard_map/pallas_call | solution.py:67
  168.3 0.7 copy.49
  169.0 0.8 copy.59
  169.9 15.5 %convolution_negate_fusion = f32[80,2048]{1,0:T(8,128)S(1)} fusion(bf16[80,8192]{1,0:T(8,128)(2,1)S(1)} %bitcast.129, bf16[2048,8192]{1,0:T(8,128)(2,1)} %param.18), kind=kOutput, calls=%fused_computation.10 | convolution fusion | flops 2684518400 | bytes 35520512 | tf_op jit(solution)/shard_map/rd,vd->rv/dot_general | solution.py:80
  185.6 1.3 copy.50
  (66 shorter events, 5.7 us)
Async XLA Ops:
  0.0 49.7 %copy-start = (bf16[2048,128]{1,0:T(8,128)(2,1)S(1)}, bf16[2048,128]{1,0:T(8,128)(2,1)}, u32[]{:S(2)}) copy-start(bf16[2048,128]{1,0:T(8,128)(2,1)} %param.14) | copy-start | bytes 1572868
  9.5 0.7 copy-start.2
  49.0 1.3 copy-start.6
  49.7 2.2 %copy-start.4 = (bf16[2048,1024]{1,0:T(8,128)(2,1)S(1)}, bf16[2048,1024]{1,0:T(8,128)(2,1)}, u32[]{:S(2)}) copy-start(bf16[2048,1024]{1,0:T(8,128)(2,1)} %param.12) | copy-start | bytes 12582916
  53.3 2.2 %copy-start.8 = (bf16[1024,2048]{1,0:T(8,128)(2,1)S(1)}, bf16[1024,2048]{1,0:T(8,128)(2,1)}, u32[]{:S(2)}) copy-start(bf16[1024,2048]{1,0:T(8,128)(2,1)} %param.15) | copy-start | bytes 12582916
  92.6 6.3 %copy-start.3 = (s32[1,20]{1,0:T(1,128)S(1)}, s32[1,20]{1,0:T(1,128)}, u32[]{:S(2)}) copy-start(s32[1,20]{1,0:T(1,128)} %refs_2_.1) | copy-start | bytes 244
  106.1 18.4 %copy-start.5 = (f32[80,2048]{1,0:T(8,128)S(1)}, f32[80,2048]{1,0:T(8,128)}, u32[]{:S(2)}) copy-start(f32[80,2048]{1,0:T(8,128)} %reshape.101) | copy-start | bytes 1966084
  169.9 15.6 %copy-start.7 = (s32[2048]{0:T(1024)S(1)}, s32[2048]{0:T(1024)}, u32[]{:S(2)}) copy-start(s32[2048]{0:T(1024)} %param.19) | copy-start | bytes 24580
  169.9 17.0 %copy-start.1 = (bf16[2048,128]{1,0:T(8,128)(2,1)S(1)}, bf16[2048,128]{1,0:T(8,128)(2,1)}, u32[]{:S(2)}) copy-start(bf16[2048,128]{1,0:T(8,128)(2,1)} %param.14) | copy-start | bytes 1572868

commit v3 on v2

--- a/solution.py
+++ b/solution.py
@@ -80,6 +80,159 @@
     return jnp.einsum(spec, a, b, preferred_element_type=jnp.float32)
 
 
+MESH = pl.DeviceIdType.MESH
+
+
+def greet(axis, peers):
+    barrier = pltpu.get_barrier_semaphore()
+    for peer in peers:
+        pl.semaphore_signal(barrier, inc=1, device_id={axis: peer}, device_id_type=MESH)
+    pl.semaphore_wait(barrier, len(peers))
+
+
+def gather_kernel(axis, count, arrays, *refs):
+    sources, targets = refs[:arrays], refs[arrays : 2 * arrays]
+    send_sem, recv_sem, own_sem = refs[2 * arrays :]
+    here = lax.axis_index(axis)
+    chips = count // 2
+    chip, core = here // 2, lax.rem(here, 2)
+    pair = 2 * chip + (1 - core)
+    kept = []
+    for i in range(arrays):
+        copy = pltpu.make_async_copy(sources[i], targets[i].at[here], own_sem.at[i])
+        copy.start()
+        kept.append(copy)
+
+    def push(i, source, slot, number, peer):
+        return pltpu.make_async_remote_copy(
+            src_ref=source,
+            dst_ref=targets[i].at[slot],
+            send_sem=send_sem.at[i, number],
+            recv_sem=recv_sem.at[i, number],
+            device_id={axis: peer},
+            device_id_type=MESH,
+        )
+
+    others = [2 * lax.rem(chip + step, chips) + core for step in range(1, chips)]
+    greet(axis, others + [pair])
+    first = []
+    for step in range(1, chips):
+        for i in range(arrays):
+            copy = push(i, sources[i], here, step, others[step - 1])
+            copy.start()
+            first.append(copy)
+    rest = []
+    for i in range(arrays):
+        copy = push(i, sources[i], here, 0, pair)
+        copy.start()
+        rest.append(copy)
+    for step in range(1, chips):
+        slot = 2 * lax.rem(chip + chips - step, chips) + core
+        for i in range(arrays):
+            first[(step - 1) * arrays + i].wait_recv()
+            copy = push(i, targets[i].at[slot], slot, chips - 1 + step, pair)
+            copy.start()
+            rest.append(copy)
+    for copy in first:
+        copy.wait_send()
+    for copy in kept + rest:
+        copy.wait()
+
+
+def gather(axis, number, *arrays):
+    count = lax.axis_size(axis)
+    shapes = [jax.ShapeDtypeStruct((count,) + a.shape, a.dtype) for a in arrays]
+    space = pl.BlockSpec(memory_space=pltpu.VMEM)
+    sems = pltpu.SemaphoreType.DMA((len(arrays), count - 1))
+    return pl.pallas_call(
+        functools.partial(gather_kernel, axis, count, len(arrays)),
+        out_shape=shapes,
+        in_specs=[space] * len(arrays),
+        out_specs=[space] * len(arrays),
+        scratch_shapes=[sems, sems, pltpu.SemaphoreType.DMA((len(arrays),))],
+        compiler_params=pltpu.CompilerParams(
+            collective_id=number, has_side_effects=True, vmem_limit_bytes=40 << 20
+        ),
+    )(*arrays)
+
+
+def line_kernel(axis, source, target, relay, send_sem, recv_sem, own_sem):
+    here = lax.axis_index(axis)
+    own = pltpu.make_async_copy(source.at[here], target.at[here], own_sem.at[0])
+    own.start()
+    greet(axis, [lax.rem(here + step, 4) for step in range(1, 4)])
+
+    def push(block, slot, number, peer, into=None):
+        return pltpu.make_async_remote_copy(
+            src_ref=block,
+            dst_ref=target.at[slot] if into is None else into,
+            send_sem=send_sem.at[number],
+            recv_sem=recv_sem.at[slot if into is None else 4],
+            device_id={axis: peer},
+            device_id_type=MESH,
+        )
+
+    for role in range(4):
+        far = 3 if role < 2 else 0
+        middle = 1 if role < 2 else 2
+        across = 3 - middle
+
+        @pl.when(here == role)
+        def _():
+            if role == middle:
+                sent = [
+                    push(source.at[across], role, 0, across),
+                    push(source.at[3 - far], role, 1, 3 - far),
+                ]
+                for copy in sent:
+                    copy.start()
+                total = push(relay, role, 2, far)
+                push(source.at[far], role, 3, far, relay).wait_recv()
+                relay[...] = relay[...] + source[far]
+                total.start()
+                sent.append(total)
+                arriving = [0, across, 3]
+            else:
+                handed = push(source.at[far], role, 0, middle, relay)
+                handed.start()
+                target[far] = jnp.zeros_like(target[far])
+                handed.wait_send()
+                sent = [
+                    push(source.at[across], role, 1, across),
+                    push(source.at[middle], role, 2, middle),
+                ]
+                for copy in sent:
+                    copy.start()
+                arriving = [1, 2]
+            for slot in arriving:
+                push(source.at[slot], slot, 3, slot).wait_recv()
+            for copy in sent:
+                copy.wait_send()
+
+    own.wait()
+
+
+def line_exchange(axis, number, blocks):
+    if lax.axis_size(axis) != 4:
+        return exchange(axis, number, (blocks, True))[0]
+    space = pl.BlockSpec(memory_space=pltpu.VMEM)
+    return pl.pallas_call(
+        functools.partial(line_kernel, axis),
+        out_shape=jax.ShapeDtypeStruct(blocks.shape, blocks.dtype),
+        in_specs=[space],
+        out_specs=space,
+        scratch_shapes=[
+            pltpu.VMEM(blocks.shape[1:], blocks.dtype),
+            pltpu.SemaphoreType.DMA((4,)),
+            pltpu.SemaphoreType.DMA((5,)),
+            pltpu.SemaphoreType.DMA((1,)),
+        ],
+        compiler_params=pltpu.CompilerParams(
+            collective_id=number, has_side_effects=True, vmem_limit_bytes=40 << 20
+        ),
+    )(blocks)
+
+
 def on_device(
     embeds,
     norm_gain,
@@ -123,7 +276,7 @@
     both, inverse_norm, suffix_all = exchange(
         "prompt", 1, (both, True), (inverse_norm, False), (suffix_pos, False)
     )
-    both, inverse_norm = exchange("tensor", 2, (both, False), (inverse_norm, False))
+    both, inverse_norm = gather("tensor", 2, both, inverse_norm)
     suffix_all = suffix_all.reshape(n_prompt, suffix_count)
     both = both.reshape(n_tensor, n_prompt, ratio, 2, split_rows, feature_cols)
     both = both.transpose(3, 1, 0, 4, 2, 5).reshape(2, n_prompt, seq_len, rows_here)
@@ -139,16 +292,16 @@
             dot_f32("psd,dc->psc", normed, query_weight),
             dot_f32("psd,dc->psc", normed, key_weight),
             dot_f32("psd,dc->psc", normed, value_weight),
+            dot_f32("psd,cd->psc", out_grad, out_weight),
         ],
         axis=2,
     )
-    context_parts = dot_f32("psd,cd->psc", out_grad, out_weight).astype(jnp.bfloat16)
-    parts, context_parts = exchange("prompt", 3, (parts, True), (context_parts, True))
+    parts = line_exchange("prompt", 3, parts)
     whole = jnp.sum(parts, axis=0).astype(jnp.bfloat16)
-    contexts = jnp.sum(context_parts.astype(jnp.float32), axis=0).astype(jnp.bfloat16)
+    contexts = whole[:, head_cols + 2 * key_cols :]
     contexts = contexts.reshape(seq_len, heads_here, HD)
     queries = whole[:, :head_cols].reshape(seq_len, heads_here, HD)
-    (key_values,) = exchange("tensor", 4, (whole[:, head_cols:], False))
+    (key_values,) = gather("tensor", 4, whole[:, head_cols : head_cols + 2 * key_cols])
     key_values = key_values.reshape(n_tensor, seq_len, 2, key_cols).transpose(2, 1, 0, 3)
     key_values = key_values.reshape(2, seq_len, KVH * HD)
     fold = min(heads_here, KVH)
@@ -215,7 +368,7 @@
     scaled = lax.dynamic_slice_in_dim(scaled, here_tensor * slice_width, slice_width, 1)
     suffix_grad = (norm_rows * (weighted - scaled * inner)).astype(jnp.bfloat16)
     (suffix_grad,) = exchange("prompt", 9, (suffix_grad, False))
-    (suffix_grad,) = exchange("tensor", 10, (suffix_grad, False))
+    (suffix_grad,) = gather("tensor", 10, suffix_grad)
     flat_grads = suffix_grad.transpose(2, 1, 0, 3).reshape(rows, width)
     scores = -dot_f32("rd,vd->rv", flat_grads, vocab_table)
     scores = scores.reshape(n_prompt, suffix_count, vocab_table.shape[0])

time: 188 us -> 171 us (0.910)
  Pallas kernels: 149 us -> 133 us
  matrix products: 25.2 us -> 27.7 us
  local copies, waits for them, and re-layouts: 8.87 us -> 6.83 us
    pallas_call x11 -> x7, Pallas kernels: 149 us -> 54.7 us  [exchange(): pl.pallas_call(functools.partial(exchange_kernel, axis, count, spread), o...]
    pallas_call x0 -> x4, Pallas kernels: none -> 78.2 us  [the longest x1 43.5 us: line_exchange(): pl.pallas_call(functools.partial(line_kernel, axis), out_shape=jax.ShapeD...]
    dot_general x14, matrix products: 25.2 us -> 27.7 us  [dot_f32(): return jnp.einsum(spec, a, b, preferred_element_type=jnp.float32)]
    unnamed x21 -> x22, local copies, waits for them, and re-layouts: 4.72 us -> 2.7 us
where the time goes in v3:
time: 171 us
  Pallas kernels  133 us (78%)
  matrix products  27.7 us (16%)
  local copies, waits for them, and re-layouts  6.83 us (4%)
  other arithmetic  2.83 us (2%)
    pallas_call x7, Pallas kernels, exchange(): pl.pallas_call(functools.partial(exchange_kernel, axis, count, spread), o...  54.7 us
    pallas_call x1, Pallas kernels, line_exchange(): pl.pallas_call(functools.partial(line_kernel, axis), out_shape=jax.ShapeD...  43.5 us
    pallas_call x3, Pallas kernels, gather(): pl.pallas_call(functools.partial(gather_kernel, axis, count, len(arrays))...  34.7 us
    dot_general x14, matrix products, dot_f32(): return jnp.einsum(spec, a, b, preferred_element_type=jnp.float32)  27.7 us

profile of v3, /device:TPU:0, one launch (start us, length us, event | category | flops | bytes accessed | tf_op | source)
XLA Modules:
  0.0 170.7 jit_solution(18245550406550278293)
XLA Ops:
  0.0 1.0 pad_maximum_fusion.1.refs_0_
  1.0 8.1 %shard_map.100 = bf16[8,16,1024]{2,1,0:T(8,128)(2,1)S(1)} custom-call(bf16[8,16,1024]{2,1,0:T(8,128)(2,1)S(1)} %pad_maximum_fusion.1.refs_0_), custom_call_target="tpu_custom_call" | custom-call | tf_op jit(solution)/shard_map/pallas_call | solution.py:67
  9.5 0.7 copy-done.2
  10.1 9.7 %shard_map.101 = (bf16[4,2,16,1024]{3,2,1,0:T(8,128)(2,1)S(1)}, f32[4,8,128]{2,1,0:T(8,128)S(1)}, s32[4,1,20]{2,1,0:T(1,128)S(1)}) custom-call(bf16[4,2,16,1024]{3,2,1,0:T(8,128)(2,1)S(1)} %bitcast.109, f32[8,128]{1,0:T(8,128)S(1)} %broadcast_in_dim.58.refs_1_, s32[1,20]{1,0:T(1,128)S(1)} %copy-done.2), custom_call_target="tpu_custom_call" | custom-call | tf_op jit(solution)/shard_map/pallas_call | solution.py:67
  19.8 17.1 %shard_map.102 = (bf16[8,4,2,16,1024]{4,3,2,1,0:T(8,128)(2,1)S(1)}, f32[8,4,8,128]{3,2,1,0:T(8,128)S(1)}) custom-call(bf16[4,2,16,1024]{3,2,1,0:T(8,128)(2,1)S(1)} %get-tuple-element.13.refs_0_, f32[4,8,128]{2,1,0:T(8,128)S(1)} %get-tuple-element.14.refs_1_), custom_call_target="tpu_custom_call" | custom-call | tf_op jit(solution)/shard_map/pallas_call | solution.py:147
  38.1 0.9 reshape.101
  39.0 0.7 dynamic-slice_convert_fusion
  39.7 3.6 %fusion.2 = f32[4,64,1024]{2,1,0:T(8,128)S(1)} fusion(bf16[4,64,2048]{2,1,0:T(8,128)(2,1)S(1)} %bitcast.125, bf16[1024,2048]{1,0:T(8,128)(2,1)} %param.15), kind=kOutput, calls=%fused_computation.2 | convolution fusion | flops 1073741824 | bytes 6291456 | tf_op jit(solution)/shard_map/psd,cd->psc/dot_general | solution.py:80
  43.9 0.5 fusion.19
  44.5 1.1 copy-done.4
  45.6 1.3 fusion.4
  47.1 43.5 %shard_map.103 = f32[4,64,2304]{2,1,0:T(8,128)S(1)} custom-call(f32[4,64,2304]{2,1,0:T(8,128)S(1)} %pad_maximum_fusion.source), custom_call_target="tpu_custom_call" | custom-call | tf_op jit(solution)/shard_map/pallas_call | solution.py:219
  90.8 6.2 %shard_map.104 = bf16[8,64,256]{2,1,0:T(8,128)(2,1)S(1)} custom-call(bf16[64,256]{1,0:T(8,128)(2,1)S(1)} %slice.62.refs_0_), custom_call_target="tpu_custom_call" | custom-call | tf_op jit(solution)/shard_map/pallas_call | solution.py:147
  98.5 5.4 %shard_map.105 = f32[8,40,128]{2,1,0:T(8,128)S(1)} custom-call(f32[8,40,128]{2,1,0:T(8,128)S(1)} %bitcast.110), custom_call_target="tpu_custom_call" | custom-call | tf_op jit(solution)/shard_map/pallas_call | solution.py:67
  104.4 8.7 %shard_map.106 = bf16[4,20,1280]{2,1,0:T(8,128)(2,1)S(1)} custom-call(bf16[20,1280]{1,0:T(8,128)(2,1)S(1)} %pad_maximum_fusion.3.refs_0_), custom_call_target="tpu_custom_call" | custom-call | tf_op jit(solution)/shard_map/pallas_call | solution.py:67
  113.8 3.8 %multiply_reduce_fusion = (f32[80]{0:T(128)S(1)}, f32[80,2048]{1,0:T(8,128)S(1)}) fusion(f32[80,2048]{1,0:T(8,128)S(1)} %copy-done.5, f32[2048]{0:T(1024)S(1)} %dynamic-slice_convert_fusion, f32[80,2048]{1,0:T(8,128)S(1)} %fusion.48, f32[80,2048]{1,0:T(8,128)S(1)} %fusion.50, bf16[2048,1024]{1,0:T(8,128)(2,1)} %param.12, bf16[80,1280]{1,0:T(8,128)(2,1)S(1)} %reshape.99), kind=kOutput, calls=%fused_computation.31 | convolution fusion | flops 336363456 | bytes 6988096 | tf_op jit(solution)/shard_map/nc,dc->nd/dot_general | solution.py:80
  117.6 10.0 %shard_map.107 = (f32[8,80,256]{2,1,0:T(8,128)S(1)}, f32[8,1,80]{2,1,0:T(1,128)S(1)}) custom-call(f32[8,80,256]{2,1,0:T(8,128)S(1)} %bitcast.107, f32[1,80]{1,0:T(1,128)S(1)} %bitcast.114), custom_call_target="tpu_custom_call" | custom-call | tf_op jit(solution)/shard_map/pallas_call | solution.py:67
  127.7 5.4 %shard_map.108 = f32[4,1,80]{2,1,0:T(1,128)S(1)} custom-call(f32[1,80]{1,0:T(1,128)S(1)} %bitcast.113), custom_call_target="tpu_custom_call" | custom-call | tf_op jit(solution)/shard_map/pallas_call | solution.py:67
  133.3 7.4 %shard_map.109.refs_0_ = bf16[4,80,256]{2,1,0:T(8,128)(2,1)S(1)} custom-call(bf16[80,256]{1,0:T(8,128)(2,1)S(1)} %multiply_convert_fusion.4.refs_0_), custom_call_target="tpu_custom_call" | custom-call | tf_op jit(solution)/shard_map/pallas_call | solution.py:67
  140.7 11.4 %shard_map.110 = bf16[8,4,80,256]{3,2,1,0:T(8,128)(2,1)S(1)} custom-call(bf16[4,80,256]{2,1,0:T(8,128)(2,1)S(1)} %shard_map.109.refs_0_), custom_call_target="tpu_custom_call" | custom-call | tf_op jit(solution)/shard_map/pallas_call | solution.py:147
  152.1 0.7 copy.51
  152.8 0.8 copy.61
  153.7 15.5 %convolution_negate_fusion = f32[80,2048]{1,0:T(8,128)S(1)} fusion(bf16[80,8192]{1,0:T(8,128)(2,1)S(1)} %bitcast.118, bf16[2048,8192]{1,0:T(8,128)(2,1)} %param.18), kind=kOutput, calls=%fused_computation.10 | convolution fusion | flops 2684518400 | bytes 35520512 | tf_op jit(solution)/shard_map/rd,vd->rv/dot_general | solution.py:80
  169.4 1.3 copy.52
  (66 shorter events, 5.3 us)
Async XLA Ops:
  0.0 43.4 %copy-start = (bf16[2048,128]{1,0:T(8,128)(2,1)S(1)}, bf16[2048,128]{1,0:T(8,128)(2,1)}, u32[]{:S(2)}) copy-start(bf16[2048,128]{1,0:T(8,128)(2,1)} %param.14) | copy-start | bytes 1572868
  9.5 0.7 copy-start.2
  39.7 4.2 %copy-start.6 = (bf16[2048,128]{1,0:T(8,128)(2,1)S(1)}, bf16[2048,128]{1,0:T(8,128)(2,1)}, u32[]{:S(2)}) copy-start(bf16[2048,128]{1,0:T(8,128)(2,1)} %param.13) | copy-start | bytes 1572868
  43.4 2.2 %copy-start.4 = (bf16[2048,1024]{1,0:T(8,128)(2,1)S(1)}, bf16[2048,1024]{1,0:T(8,128)(2,1)}, u32[]{:S(2)}) copy-start(bf16[2048,1024]{1,0:T(8,128)(2,1)} %param.12) | copy-start | bytes 12582916
  90.6 6.8 %copy-start.3 = (s32[1,20]{1,0:T(1,128)S(1)}, s32[1,20]{1,0:T(1,128)}, u32[]{:S(2)}) copy-start(s32[1,20]{1,0:T(1,128)} %refs_2_.1) | copy-start | bytes 244
  98.5 15.0 %copy-start.7 = (bf16[2048,128]{1,0:T(8,128)(2,1)S(1)}, bf16[2048,128]{1,0:T(8,128)(2,1)}, u32[]{:S(2)}) copy-start(bf16[2048,128]{1,0:T(8,128)(2,1)} %param.13) | copy-start | bytes 1572868
  104.0 9.8 %copy-start.5 = (f32[80,2048]{1,0:T(8,128)S(1)}, f32[80,2048]{1,0:T(8,128)}, u32[]{:S(2)}) copy-start(f32[80,2048]{1,0:T(8,128)} %reshape.101) | copy-start | bytes 1966084
  153.7 15.6 %copy-start.8 = (s32[2048]{0:T(1024)S(1)}, s32[2048]{0:T(1024)}, u32[]{:S(2)}) copy-start(s32[2048]{0:T(1024)} %param.19) | copy-start | bytes 24580
  153.7 17.0 %copy-start.1 = (bf16[2048,128]{1,0:T(8,128)(2,1)S(1)}, bf16[2048,128]{1,0:T(8,128)(2,1)}, u32[]{:S(2)}) copy-start(bf16[2048,128]{1,0:T(8,128)(2,1)} %param.14) | copy-start | bytes 1572868

commit v4 on v3

--- a/solution.py
+++ b/solution.py
@@ -231,6 +231,66 @@
             collective_id=number, has_side_effects=True, vmem_limit_bytes=40 << 20
         ),
     )(blocks)
+
+
+CHUNK = 256
+
+
+def score_kernel(
+    axis, count, part, vocab, scores, got, flat, table, send_sem, recv_sem, own_sem, load_sem
+):
+    def load(c):
+        span = pl.ds(pl.multiple_of(c * CHUNK, CHUNK), CHUNK)
+        return pltpu.make_async_copy(vocab.at[span], table.at[span], load_sem.at[c])
+
+    chunks = vocab.shape[0] // CHUNK
+    for c in range(chunks):
+        load(c).start()
+    gather_kernel(axis, count, 1, part, got, send_sem, recv_sem, own_sem)
+    wide = part.shape[2]
+    for p in range(part.shape[0]):
+        for t in range(count):
+            start = (p * count + t) * wide
+            flat[:, start : start + wide] = got[t, p]
+
+    @pl.loop(0, chunks)
+    def _(c):
+        load(c).wait()
+        span = pl.ds(pl.multiple_of(c * CHUNK, CHUNK), CHUNK)
+        scores[:, span] = -lax.dot_general(
+            flat[...],
+            table[span, :],
+            (((1,), (1,)), ((), ())),
+            preferred_element_type=jnp.float32,
+        )
+
+
+def gather_score(axis, number, part, vocab):
+    count = lax.axis_size(axis)
+    n_prompt, rows, wide = part.shape
+    vocab_here, width = vocab.shape
+    if wide % 128 or vocab_here % CHUNK or rows % 16:
+        (part,) = gather(axis, number, part)
+        return -dot_f32("rd,vd->rv", part.transpose(2, 1, 0, 3).reshape(rows, width), vocab)
+    sems = pltpu.SemaphoreType.DMA((1, count - 1))
+    return pl.pallas_call(
+        functools.partial(score_kernel, axis, count),
+        out_shape=jax.ShapeDtypeStruct((rows, vocab_here), jnp.float32),
+        in_specs=[pl.BlockSpec(memory_space=pltpu.VMEM), pl.BlockSpec(memory_space=pl.ANY)],
+        out_specs=pl.BlockSpec(memory_space=pltpu.VMEM),
+        scratch_shapes=[
+            pltpu.VMEM((count,) + part.shape, part.dtype),
+            pltpu.VMEM((rows, width), part.dtype),
+            pltpu.VMEM(vocab.shape, vocab.dtype),
+            sems,
+            sems,
+            pltpu.SemaphoreType.DMA((1,)),
+            pltpu.SemaphoreType.DMA((vocab_here // CHUNK,)),
+        ],
+        compiler_params=pltpu.CompilerParams(
+            collective_id=number, has_side_effects=True, vmem_limit_bytes=52 << 20
+        ),
+    )(part, vocab)
 
 
 def on_device(
@@ -368,9 +428,7 @@
     scaled = lax.dynamic_slice_in_dim(scaled, here_tensor * slice_width, slice_width, 1)
     suffix_grad = (norm_rows * (weighted - scaled * inner)).astype(jnp.bfloat16)
     (suffix_grad,) = exchange("prompt", 9, (suffix_grad, False))
-    (suffix_grad,) = gather("tensor", 10, suffix_grad)
-    flat_grads = suffix_grad.transpose(2, 1, 0, 3).reshape(rows, width)
-    scores = -dot_f32("rd,vd->rv", flat_grads, vocab_table)
+    scores = gather_score("tensor", 10, suffix_grad, vocab_table)
     scores = scores.reshape(n_prompt, suffix_count, vocab_table.shape[0])
     return jnp.where(banned[None, None, :] == 1, 0.0, scores)
 

time: 171 us -> 165 us (0.965)
  matrix products: 27.7 us -> 12.1 us
  Pallas kernels: 133 us -> 144 us
    pallas_call x0 -> x1, Pallas kernels: none -> 22.9 us  [gather_score(): pl.pallas_call(functools.partial(score_kernel, axis, count), out_shape=ja...]
    dot_general x14 -> x13, matrix products: 27.7 us -> 12.1 us  [dot_f32(): return jnp.einsum(spec, a, b, preferred_element_type=jnp.float32)]
    pallas_call x3 -> x2, Pallas kernels: 34.7 us -> 23.3 us  [gather(): pl.pallas_call(functools.partial(gather_kernel, axis, count, len(arrays))...]
where the time goes in v4:
time: 165 us
  Pallas kernels  144 us (87%)
  matrix products  12.1 us (7%)
  local copies, waits for them, and re-layouts  5.26 us (3%)
  other arithmetic  2.83 us (2%)
    pallas_call x7, Pallas kernels, exchange(): pl.pallas_call(functools.partial(exchange_kernel, axis, count, spread), o...  54.7 us
    pallas_call x1, Pallas kernels, line_exchange(): pl.pallas_call(functools.partial(line_kernel, axis), out_shape=jax.ShapeD...  43.5 us
    pallas_call x2, Pallas kernels, gather(): pl.pallas_call(functools.partial(gather_kernel, axis, count, len(arrays))...  23.3 us
    pallas_call x1, Pallas kernels, gather_score(): pl.pallas_call(functools.partial(score_kernel, axis, count), out_shape=ja...  22.9 us
    dot_general x13, matrix products, dot_f32(): return jnp.einsum(spec, a, b, preferred_element_type=jnp.float32)  12.1 us

profile of v4, /device:TPU:0, one launch (start us, length us, event | category | flops | bytes accessed | tf_op | source)
XLA Modules:
  0.0 165.0 jit_solution(464761288042672808)
XLA Ops:
  0.0 1.0 pad_maximum_fusion.1.refs_0_
  1.0 8.1 %shard_map.100 = bf16[8,16,1024]{2,1,0:T(8,128)(2,1)S(1)} custom-call(bf16[8,16,1024]{2,1,0:T(8,128)(2,1)S(1)} %pad_maximum_fusion.1.refs_0_), custom_call_target="tpu_custom_call" | custom-call | tf_op jit(solution)/shard_map/pallas_call | solution.py:67
  9.5 0.7 copy-done.2
  10.1 9.7 %shard_map.101 = (bf16[4,2,16,1024]{3,2,1,0:T(8,128)(2,1)S(1)}, f32[4,8,128]{2,1,0:T(8,128)S(1)}, s32[4,1,20]{2,1,0:T(1,128)S(1)}) custom-call(bf16[4,2,16,1024]{3,2,1,0:T(8,128)(2,1)S(1)} %bitcast.102, f32[8,128]{1,0:T(8,128)S(1)} %broadcast_in_dim.58.refs_1_, s32[1,20]{1,0:T(1,128)S(1)} %copy-done.2), custom_call_target="tpu_custom_call" | custom-call | tf_op jit(solution)/shard_map/pallas_call | solution.py:67
  19.8 17.1 %shard_map.102 = (bf16[8,4,2,16,1024]{4,3,2,1,0:T(8,128)(2,1)S(1)}, f32[8,4,8,128]{3,2,1,0:T(8,128)S(1)}) custom-call(bf16[4,2,16,1024]{3,2,1,0:T(8,128)(2,1)S(1)} %get-tuple-element.13.refs_0_, f32[4,8,128]{2,1,0:T(8,128)S(1)} %get-tuple-element.14.refs_1_), custom_call_target="tpu_custom_call" | custom-call | tf_op jit(solution)/shard_map/pallas_call | solution.py:147
  38.0 0.9 reshape.98
  38.9 0.7 dynamic-slice_convert_fusion
  39.7 3.6 %fusion.2 = f32[4,64,1024]{2,1,0:T(8,128)S(1)} fusion(bf16[4,64,2048]{2,1,0:T(8,128)(2,1)S(1)} %bitcast.116, bf16[1024,2048]{1,0:T(8,128)(2,1)} %param.15), kind=kOutput, calls=%fused_computation.2 | convolution fusion | flops 1073741824 | bytes 6291456 | tf_op jit(solution)/shard_map/psd,cd->psc/dot_general | solution.py:80
  43.4 0.5 fusion.18
  43.9 0.5 fusion.19
  44.4 1.1 copy-done.4
  45.6 1.3 fusion.4
  47.1 43.5 %shard_map.103 = f32[4,64,2304]{2,1,0:T(8,128)S(1)} custom-call(f32[4,64,2304]{2,1,0:T(8,128)S(1)} %pad_maximum_fusion.source), custom_call_target="tpu_custom_call" | custom-call | tf_op jit(solution)/shard_map/pallas_call | solution.py:219
  90.8 6.2 %shard_map.104 = bf16[8,64,256]{2,1,0:T(8,128)(2,1)S(1)} custom-call(bf16[64,256]{1,0:T(8,128)(2,1)S(1)} %slice.62.refs_0_), custom_call_target="tpu_custom_call" | custom-call | tf_op jit(solution)/shard_map/pallas_call | solution.py:147
  98.0 0.3 convolution_bitcast_fusion.1
  98.5 5.4 %shard_map.105 = f32[8,40,128]{2,1,0:T(8,128)S(1)} custom-call(f32[8,40,128]{2,1,0:T(8,128)S(1)} %bitcast.103), custom_call_target="tpu_custom_call" | custom-call | tf_op jit(solution)/shard_map/pallas_call | solution.py:67
  104.0 0.4 fusion.15
  104.4 8.7 %shard_map.106 = bf16[4,20,1280]{2,1,0:T(8,128)(2,1)S(1)} custom-call(bf16[20,1280]{1,0:T(8,128)(2,1)S(1)} %pad_maximum_fusion.3.refs_0_), custom_call_target="tpu_custom_call" | custom-call | tf_op jit(solution)/shard_map/pallas_call | solution.py:67
  113.7 3.8 %multiply_reduce_fusion = (f32[80]{0:T(128)S(1)}, f32[80,2048]{1,0:T(8,128)S(1)}) fusion(f32[80,2048]{1,0:T(8,128)S(1)} %copy-done.5, f32[2048]{0:T(1024)S(1)} %dynamic-slice_convert_fusion, f32[80,2048]{1,0:T(8,128)S(1)} %fusion.48, f32[80,2048]{1,0:T(8,128)S(1)} %fusion.50, bf16[2048,1024]{1,0:T(8,128)(2,1)} %param.12, bf16[80,1280]{1,0:T(8,128)(2,1)S(1)} %reshape.96), kind=kOutput, calls=%fused_computation.30 | convolution fusion | flops 336363456 | bytes 6988096 | tf_op jit(solution)/shard_map/nc,dc->nd/dot_general | solution.py:80
  117.6 10.0 %shard_map.107 = (f32[8,80,256]{2,1,0:T(8,128)S(1)}, f32[8,1,80]{2,1,0:T(1,128)S(1)}) custom-call(f32[8,80,256]{2,1,0:T(8,128)S(1)} %bitcast.100, f32[1,80]{1,0:T(1,128)S(1)} %bitcast.107), custom_call_target="tpu_custom_call" | custom-call | tf_op jit(solution)/shard_map/pallas_call | solution.py:67
  127.7 5.4 %shard_map.108 = f32[4,1,80]{2,1,0:T(1,128)S(1)} custom-call(f32[1,80]{1,0:T(1,128)S(1)} %bitcast.106), custom_call_target="tpu_custom_call" | custom-call | tf_op jit(solution)/shard_map/pallas_call | solution.py:67
  133.3 7.4 %shard_map.109.part = bf16[4,80,256]{2,1,0:T(8,128)(2,1)S(1)} custom-call(bf16[80,256]{1,0:T(8,128)(2,1)S(1)} %multiply_convert_fusion.4.refs_0_), custom_call_target="tpu_custom_call" | custom-call | tf_op jit(solution)/shard_map/pallas_call | solution.py:67
  140.7 22.9 %shard_map.110 = f32[80,2048]{1,0:T(8,128)S(1)} custom-call(bf16[4,80,256]{2,1,0:T(8,128)(2,1)S(1)} %shard_map.109.part, bf16[2048,8192]{1,0:T(8,128)(2,1)} %vocab.1), custom_call_target="tpu_custom_call" | custom-call | tf_op jit(solution)/shard_map/pallas_call | solution.py:276
  163.8 1.3 copy.50
  (63 shorter events, 4.1 us)
Async XLA Ops:
  0.0 43.4 %copy-start = (bf16[2048,128]{1,0:T(8,128)(2,1)S(1)}, bf16[2048,128]{1,0:T(8,128)(2,1)}, u32[]{:S(2)}) copy-start(bf16[2048,128]{1,0:T(8,128)(2,1)} %param.14) | copy-start | bytes 1572868
  9.5 0.7 copy-start.2
  39.7 4.2 %copy-start.6 = (bf16[2048,128]{1,0:T(8,128)(2,1)S(1)}, bf16[2048,128]{1,0:T(8,128)(2,1)}, u32[]{:S(2)}) copy-start(bf16[2048,128]{1,0:T(8,128)(2,1)} %param.13) | copy-start | bytes 1572868
  43.4 2.2 %copy-start.4 = (bf16[2048,1024]{1,0:T(8,128)(2,1)S(1)}, bf16[2048,1024]{1,0:T(8,128)(2,1)}, u32[]{:S(2)}) copy-start(bf16[2048,1024]{1,0:T(8,128)(2,1)} %param.12) | copy-start | bytes 12582916
  90.6 6.8 %copy-start.3 = (s32[1,20]{1,0:T(1,128)S(1)}, s32[1,20]{1,0:T(1,128)}, u32[]{:S(2)}) copy-start(s32[1,20]{1,0:T(1,128)} %refs_2_.1) | copy-start | bytes 244
  98.5 15.0 %copy-start.7 = (bf16[2048,128]{1,0:T(8,128)(2,1)S(1)}, bf16[2048,128]{1,0:T(8,128)(2,1)}, u32[]{:S(2)}) copy-start(bf16[2048,128]{1,0:T(8,128)(2,1)} %param.13) | copy-start | bytes 1572868
  104.0 9.8 %copy-start.5 = (f32[80,2048]{1,0:T(8,128)S(1)}, f32[80,2048]{1,0:T(8,128)}, u32[]{:S(2)}) copy-start(f32[80,2048]{1,0:T(8,128)} %reshape.98) | copy-start | bytes 1966084
  140.7 23.0 %copy-start.8 = (s32[2048]{0:T(1024)S(1)}, s32[2048]{0:T(1024)}, u32[]{:S(2)}) copy-start(s32[2048]{0:T(1024)} %param.19) | copy-start | bytes 24580
  140.7 24.3 %copy-start.1 = (bf16[2048,128]{1,0:T(8,128)(2,1)S(1)}, bf16[2048,128]{1,0:T(8,128)(2,1)}, u32[]{:S(2)}) copy-start(bf16[2048,128]{1,0:T(8,128)(2,1)} %param.14) | copy-start | bytes 1572868

commit v5 on v4

--- a/solution.py
+++ b/solution.py
@@ -233,7 +233,7 @@
     )(blocks)
 
 
-CHUNK = 256
+CHUNK = 512
 
 
 def score_kernel(

time: 165 us -> 165 us (level)
  no operation moved by 1% of the time
where the time goes in v5:
time: 165 us; the launch traced here: 164 us
  Pallas kernels  144 us (87%)
  matrix products  12.1 us (7%)
  local copies, waits for them, and re-layouts  5.26 us (3%)
  other arithmetic  2.83 us (2%)
    pallas_call x7, Pallas kernels, exchange(): pl.pallas_call(functools.partial(exchange_kernel, axis, count, spread), o...  54.7 us
    pallas_call x1, Pallas kernels, line_exchange(): pl.pallas_call(functools.partial(line_kernel, axis), out_shape=jax.ShapeD...  43.5 us
    pallas_call x2, Pallas kernels, gather(): pl.pallas_call(functools.partial(gather_kernel, axis, count, len(arrays))...  23.3 us
    pallas_call x1, Pallas kernels, gather_score(): pl.pallas_call(functools.partial(score_kernel, axis, count), out_shape=ja...  22.2 us
    dot_general x13, matrix products, dot_f32(): return jnp.einsum(spec, a, b, preferred_element_type=jnp.float32)  12.1 us

profile of v5, /device:TPU:0, one launch (start us, length us, event | category | flops | bytes accessed | tf_op | source)
XLA Modules:
  0.0 164.4 jit_solution(8598336003031692859)
XLA Ops:
  0.0 1.0 pad_maximum_fusion.1.refs_0_
  1.0 8.1 %shard_map.100 = bf16[8,16,1024]{2,1,0:T(8,128)(2,1)S(1)} custom-call(bf16[8,16,1024]{2,1,0:T(8,128)(2,1)S(1)} %pad_maximum_fusion.1.refs_0_), custom_call_target="tpu_custom_call" | custom-call | tf_op jit(solution)/shard_map/pallas_call | solution.py:67
  9.5 0.7 copy-done.2
  10.1 9.7 %shard_map.101 = (bf16[4,2,16,1024]{3,2,1,0:T(8,128)(2,1)S(1)}, f32[4,8,128]{2,1,0:T(8,128)S(1)}, s32[4,1,20]{2,1,0:T(1,128)S(1)}) custom-call(bf16[4,2,16,1024]{3,2,1,0:T(8,128)(2,1)S(1)} %bitcast.102, f32[8,128]{1,0:T(8,128)S(1)} %broadcast_in_dim.58.refs_1_, s32[1,20]{1,0:T(1,128)S(1)} %copy-done.2), custom_call_target="tpu_custom_call" | custom-call | tf_op jit(solution)/shard_map/pallas_call | solution.py:67
  19.8 17.1 %shard_map.102 = (bf16[8,4,2,16,1024]{4,3,2,1,0:T(8,128)(2,1)S(1)}, f32[8,4,8,128]{3,2,1,0:T(8,128)S(1)}) custom-call(bf16[4,2,16,1024]{3,2,1,0:T(8,128)(2,1)S(1)} %get-tuple-element.13.refs_0_, f32[4,8,128]{2,1,0:T(8,128)S(1)} %get-tuple-element.14.refs_1_), custom_call_target="tpu_custom_call" | custom-call | tf_op jit(solution)/shard_map/pallas_call | solution.py:147
  38.0 0.9 reshape.98
  38.9 0.7 dynamic-slice_convert_fusion
  39.7 3.6 %fusion.2 = f32[4,64,1024]{2,1,0:T(8,128)S(1)} fusion(bf16[4,64,2048]{2,1,0:T(8,128)(2,1)S(1)} %bitcast.116, bf16[1024,2048]{1,0:T(8,128)(2,1)} %param.15), kind=kOutput, calls=%fused_computation.2 | convolution fusion | flops 1073741824 | bytes 6291456 | tf_op jit(solution)/shard_map/psd,cd->psc/dot_general | solution.py:80
  43.4 0.5 fusion.18
  43.9 0.5 fusion.19
  44.4 1.1 copy-done.4
  45.6 1.3 fusion.4
  47.1 43.5 %shard_map.103 = f32[4,64,2304]{2,1,0:T(8,128)S(1)} custom-call(f32[4,64,2304]{2,1,0:T(8,128)S(1)} %pad_maximum_fusion.source), custom_call_target="tpu_custom_call" | custom-call | tf_op jit(solution)/shard_map/pallas_call | solution.py:219
  90.8 6.2 %shard_map.104 = bf16[8,64,256]{2,1,0:T(8,128)(2,1)S(1)} custom-call(bf16[64,256]{1,0:T(8,128)(2,1)S(1)} %slice.62.refs_0_), custom_call_target="tpu_custom_call" | custom-call | tf_op jit(solution)/shard_map/pallas_call | solution.py:147
  98.0 0.3 convolution_bitcast_fusion.1
  98.5 5.4 %shard_map.105 = f32[8,40,128]{2,1,0:T(8,128)S(1)} custom-call(f32[8,40,128]{2,1,0:T(8,128)S(1)} %bitcast.103), custom_call_target="tpu_custom_call" | custom-call | tf_op jit(solution)/shard_map/pallas_call | solution.py:67
  104.0 0.4 fusion.15
  104.4 8.7 %shard_map.106 = bf16[4,20,1280]{2,1,0:T(8,128)(2,1)S(1)} custom-call(bf16[20,1280]{1,0:T(8,128)(2,1)S(1)} %pad_maximum_fusion.3.refs_0_), custom_call_target="tpu_custom_call" | custom-call | tf_op jit(solution)/shard_map/pallas_call | solution.py:67
  113.7 3.8 %multiply_reduce_fusion = (f32[80]{0:T(128)S(1)}, f32[80,2048]{1,0:T(8,128)S(1)}) fusion(f32[80,2048]{1,0:T(8,128)S(1)} %copy-done.5, f32[2048]{0:T(1024)S(1)} %dynamic-slice_convert_fusion, f32[80,2048]{1,0:T(8,128)S(1)} %fusion.48, f32[80,2048]{1,0:T(8,128)S(1)} %fusion.50, bf16[2048,1024]{1,0:T(8,128)(2,1)} %param.12, bf16[80,1280]{1,0:T(8,128)(2,1)S(1)} %reshape.96), kind=kOutput, calls=%fused_computation.30 | convolution fusion | flops 336363456 | bytes 6988096 | tf_op jit(solution)/shard_map/nc,dc->nd/dot_general | solution.py:80
  117.6 10.0 %shard_map.107 = (f32[8,80,256]{2,1,0:T(8,128)S(1)}, f32[8,1,80]{2,1,0:T(1,128)S(1)}) custom-call(f32[8,80,256]{2,1,0:T(8,128)S(1)} %bitcast.100, f32[1,80]{1,0:T(1,128)S(1)} %bitcast.107), custom_call_target="tpu_custom_call" | custom-call | tf_op jit(solution)/shard_map/pallas_call | solution.py:67
  127.7 5.4 %shard_map.108 = f32[4,1,80]{2,1,0:T(1,128)S(1)} custom-call(f32[1,80]{1,0:T(1,128)S(1)} %bitcast.106), custom_call_target="tpu_custom_call" | custom-call | tf_op jit(solution)/shard_map/pallas_call | solution.py:67
  133.3 7.4 %shard_map.109.part = bf16[4,80,256]{2,1,0:T(8,128)(2,1)S(1)} custom-call(bf16[80,256]{1,0:T(8,128)(2,1)S(1)} %multiply_convert_fusion.4.refs_0_), custom_call_target="tpu_custom_call" | custom-call | tf_op jit(solution)/shard_map/pallas_call | solution.py:67
  140.7 22.2 %shard_map.110 = f32[80,2048]{1,0:T(8,128)S(1)} custom-call(bf16[4,80,256]{2,1,0:T(8,128)(2,1)S(1)} %shard_map.109.part, bf16[2048,8192]{1,0:T(8,128)(2,1)} %vocab.1), custom_call_target="tpu_custom_call" | custom-call | tf_op jit(solution)/shard_map/pallas_call | solution.py:276
  163.1 1.3 copy.50
  (63 shorter events, 4.1 us)
Async XLA Ops:
  0.0 43.4 %copy-start = (bf16[2048,128]{1,0:T(8,128)(2,1)S(1)}, bf16[2048,128]{1,0:T(8,128)(2,1)}, u32[]{:S(2)}) copy-start(bf16[2048,128]{1,0:T(8,128)(2,1)} %param.14) | copy-start | bytes 1572868
  9.5 0.7 copy-start.2
  39.7 4.2 %copy-start.6 = (bf16[2048,128]{1,0:T(8,128)(2,1)S(1)}, bf16[2048,128]{1,0:T(8,128)(2,1)}, u32[]{:S(2)}) copy-start(bf16[2048,128]{1,0:T(8,128)(2,1)} %param.13) | copy-start | bytes 1572868
  43.4 2.2 %copy-start.4 = (bf16[2048,1024]{1,0:T(8,128)(2,1)S(1)}, bf16[2048,1024]{1,0:T(8,128)(2,1)}, u32[]{:S(2)}) copy-start(bf16[2048,1024]{1,0:T(8,128)(2,1)} %param.12) | copy-start | bytes 12582916
  90.6 6.8 %copy-start.3 = (s32[1,20]{1,0:T(1,128)S(1)}, s32[1,20]{1,0:T(1,128)}, u32[]{:S(2)}) copy-start(s32[1,20]{1,0:T(1,128)} %refs_2_.1) | copy-start | bytes 244
  98.5 15.0 %copy-start.7 = (bf16[2048,128]{1,0:T(8,128)(2,1)S(1)}, bf16[2048,128]{1,0:T(8,128)(2,1)}, u32[]{:S(2)}) copy-start(bf16[2048,128]{1,0:T(8,128)(2,1)} %param.13) | copy-start | bytes 1572868
  104.0 9.8 %copy-start.5 = (f32[80,2048]{1,0:T(8,128)S(1)}, f32[80,2048]{1,0:T(8,128)}, u32[]{:S(2)}) copy-start(f32[80,2048]{1,0:T(8,128)} %reshape.98) | copy-start | bytes 1966084
  140.7 22.3 %copy-start.8 = (s32[2048]{0:T(1024)S(1)}, s32[2048]{0:T(1024)}, u32[]{:S(2)}) copy-start(s32[2048]{0:T(1024)} %param.19) | copy-start | bytes 24580
  140.7 23.7 %copy-start.1 = (bf16[2048,128]{1,0:T(8,128)(2,1)S(1)}, bf16[2048,128]{1,0:T(8,128)(2,1)}, u32[]{:S(2)}) copy-start(bf16[2048,128]{1,0:T(8,128)(2,1)} %param.14) | copy-start | bytes 1572868
